TPU v7x, 32 devices: a whole 2x2x4 slice. The times are simulated.
32 devices in a mesh: lat: 8 (over y, x, core), lon: 4 (over z).
Axes of the slice: x: 2, y: 2, z: 4, core: 2. Of those that a mesh axis runs over, the one named last changes fastest.
Arguments:
- fields: bfloat16 [4, 64, 256, 640], P(None, 'lat', 'lon'), may hold values from -6 to 6
- kernel: float32 [64, 9, 3, 256], P('lat'), may hold values from -0.125 to 0.125
- theta: float32 [3, 640], P(None, 'lon'), may hold values from -4 to 4
- row_start: int32 [64], P('lat'), may hold values from 0 to 59, as said below
- row_count: int32 [64], P('lat'), may hold values from 1 to 9
- norm_gain: float32 [640], replicated, may hold values from 0.1 to 1.9
- w_in: bfloat16 [640, 1280], replicated, may hold values from -0.25 to 0.25
- b_in: float32 [1280], replicated, may hold values from -3 to 3
- w_out: bfloat16 [1280, 640], replicated, may hold values from -0.15625 to 0.15625
Outputs:
- block_out: bfloat16 [4, 64, 256, 640], P(None, 'lat', 'lon')
Inputs may be any that keep to these rules, and one draw needn't show every extreme that they name: Output row i draws on rows row_start[i] to row_start[i] + row_count[i] - 1, all inside the grid and within 4 rows of i.
All inputs are finite; a program needn't handle non-finite values.
Results may differ from a plain program's by a relative error of at most 0.0085.
Values may be sent and summed in bfloat16 or wider, within the bound.
A program may use at most 192 MiB of HBM per device.

v0:
```python
import math

import jax
import jax.numpy as jnp
from jax import lax
from jax.sharding import PartitionSpec as P

REACH = 4
SLOTS = 9


def with_halo(value, sides, width):
    for axis, dim in sides:
        size, length = (lax.axis_size(axis), value.shape[dim])
        up = [(i, (i + 1) % size) for i in range(size - 1)]
        down = [(j, i) for i, j in up]
        last = lax.slice_in_dim(value, length - width, length, axis=dim)
        initial = lax.slice_in_dim(value, 0, width, axis=dim)
        before = lax.ppermute(last, axis, up)
        after = lax.ppermute(initial, axis, down)
        value = jnp.concatenate([before, value, after], axis=dim)
    return value


def circle_tables(length):
    bins = length // 2 + 1
    points = jnp.arange(length, dtype=jnp.int32)
    freqs = jnp.arange(bins, dtype=jnp.int32)
    phase = points[:, None] * freqs[None, :] % length
    angle = phase.astype(jnp.float32) * (2.0 * math.pi / length)
    cosine = jnp.cos(angle)
    sine = jnp.sin(angle)
    onward = jnp.concatenate([cosine, -sine], axis=1)
    weight = jnp.where((freqs == 0) | (freqs == length // 2), 1.0, 2.0).astype(jnp.float32)
    backward = (
        jnp.concatenate([(cosine * weight[None, :]).T, (-sine * weight[None, :]).T], axis=0)
        / length
    )
    return (onward, backward, bins)


def forward(field, onward, bins):
    upper = onward.astype(jnp.bfloat16)
    lower = (onward - upper.astype(jnp.float32)).astype(jnp.bfloat16)
    spectrum = jnp.einsum("ejlc,lg->ejgc", field, upper, preferred_element_type=jnp.float32)
    spectrum = spectrum + jnp.einsum(
        "ejlc,lg->ejgc", field, lower, preferred_element_type=jnp.float32
    )
    return (spectrum[:, :, :bins], spectrum[:, :, bins:])


def mix_basis(kern_part, theta):
    mixed = kern_part[:, :, 0, :, None] * theta[0][None, None, None, :]
    for basis in range(1, kern_part.shape[2]):
        mixed = mixed + kern_part[:, :, basis, :, None] * theta[basis][None, None, None, :]
    return mixed


def shards(fields, kernel, theta, row_start, row_count, norm_gain, w_in, b_in, w_out):
    local = lax.all_to_all(fields, "lon", split_axis=3, concat_axis=2, tiled=True)
    members, band, circle, chans = local.shape
    onward, backward, bins = circle_tables(circle)
    widened = with_halo(local, (("lat", 1),), REACH)
    spec_re, spec_im = forward(widened, onward, bins)
    kern_all = jnp.einsum("irkm,mg->irkg", kernel, onward, precision=lax.Precision.HIGHEST)
    mixed_re = mix_basis(kern_all[..., :bins], theta)
    mixed_im = mix_basis(kern_all[..., bins:], theta)
    first_row = lax.axis_index("lat") * band - REACH
    span_rows = band + 2 * REACH
    slot_ids = jnp.arange(SLOTS, dtype=jnp.int32)
    offsets = row_start - first_row
    live_slot = slot_ids[None, :] < row_count[:, None]
    total_re = jnp.zeros((members, band, bins, chans), jnp.float32)
    total_im = jnp.zeros((members, band, bins, chans), jnp.float32)
    for span in range(span_rows):
        select = (live_slot & (offsets[:, None] + slot_ids[None, :] == span)).astype(jnp.float32)
        coef_re = jnp.einsum("is,isfc->ifc", select, mixed_re, precision=lax.Precision.HIGHEST)
        coef_im = jnp.einsum("is,isfc->ifc", select, mixed_im, precision=lax.Precision.HIGHEST)
        row_re = spec_re[:, span][:, None]
        row_im = spec_im[:, span][:, None]
        total_re = total_re + coef_re * row_re - coef_im * row_im
        total_im = total_im + coef_re * row_im + coef_im * row_re
    joined = jnp.concatenate([total_re, total_im], axis=2)
    conv = jnp.einsum("eigc,gl->eilc", joined, backward, precision=lax.Precision.HIGHEST).astype(
        jnp.bfloat16
    )
    values = lax.all_to_all(conv, "lon", split_axis=2, concat_axis=3, tiled=True).astype(
        jnp.float32
    )
    mean = jnp.mean(values, axis=-1, keepdims=True)
    var = jnp.mean((values - mean) ** 2, axis=-1, keepdims=True)
    normed = ((values - mean) * lax.rsqrt(var + 1e-05) * norm_gain).astype(jnp.bfloat16)
    hidden = jax.nn.gelu(
        jnp.einsum("eblc,ch->eblh", normed, w_in, preferred_element_type=jnp.float32) + b_in,
        approximate=False,
    ).astype(jnp.bfloat16)
    branch = jnp.einsum("eblh,hc->eblc", hidden, w_out, preferred_element_type=jnp.float32)
    return (fields.astype(jnp.float32) + branch).astype(jnp.bfloat16)


def solution(mesh):
    placed = (
        P(None, "lat", "lon", None),
        P("lat", None, None, None),
        P(None, "lon"),
        P("lat"),
        P("lat"),
        P(),
        P(),
        P(),
        P(),
    )
    return jax.shard_map(
        shards, mesh=mesh, in_specs=placed, out_specs=P(None, "lat", "lon", None), check_vma=False
    )
```

profile of v0, /device:TPU:24, one launch (start us, length us, event | category | flops | bytes accessed | tf_op | source)
XLA Modules:
  0.0 776.0 jit_solution(13815372184327773246)
XLA Ops:
  0.0 9.0 %copy.27 = bf16[4,8,64,640]{2,1,0,3:T(8,128)(2,1)} copy(bf16[4,8,64,640]{3,2,1,0:T(8,128)(2,1)} %param.9) | data formatting | bytes 5242880 | tf_op args[0]
  23.5 8.0 %multiply_add_fusion.1 = (f32[8,9,129,160]{3,2,1,0:T(8,128)S(1)}, f32[8,9,129,160]{3,2,1,0:T(8,128)S(1)}) fusion(f32[160]{0:T(256)S(1)} %bitcast.266, f32[8,9,129]{2,1,0:T(8,128)S(1)} %get-tuple-element.47, f32[160]{0:T(256)S(1)} %bitcast.267, f32[8,9,129]{2,1,0:T(8,128)S(1)} %get-tuple-element.48, f32[160]{0:T(256)S(1)} %bitcast.265, ...), kind=kLoop, calls=%fused_computation.88 | loop fusion | flops 14860800 | bytes 12113472 | tf_op jit(solution)/shard_map/add | solution.py:55
  31.5 9.5 %fusion.62 = f32[8,1,129,160]{3,1,2,0:T(1,128)} fusion(f32[8,9,129,160]{3,2,1,0:T(8,128)S(1)} %get-tuple-element.52, pred[8,9,1,1]{1,0,2,3:T(8,128)(4,1)S(1)} %get-tuple-element.56), kind=kOutput, calls=%fused_computation.62 | convolution fusion | flops 17832960 | bytes 6604872 | tf_op jit(solution)/shard_map/is,isfc->ifc/dot_general | solution.py:77
  41.0 9.6 %fusion.30 = f32[8,1,129,160]{3,1,2,0:T(1,128)} fusion(f32[8,9,129,160]{3,2,1,0:T(8,128)S(1)} %get-tuple-element.53, pred[8,9,1,1]{1,0,2,3:T(8,128)(4,1)S(1)} %get-tuple-element.56), kind=kOutput, calls=%fused_computation.30 | convolution fusion | flops 17832960 | bytes 6604872 | tf_op jit(solution)/shard_map/is,isfc->ifc/dot_general | solution.py:78
  50.7 9.5 %fusion.60 = f32[8,1,129,160]{3,1,2,0:T(1,128)} fusion(f32[8,9,129,160]{3,2,1,0:T(8,128)S(1)} %get-tuple-element.52, pred[8,9,1,1]{1,0,2,3:T(8,128)(4,1)S(1)} %get-tuple-element.71), kind=kOutput, calls=%fused_computation.60 | convolution fusion | flops 17832960 | bytes 6604872 | tf_op jit(solution)/shard_map/is,isfc->ifc/dot_general | solution.py:77
  60.2 9.7 %fusion.28 = f32[8,1,129,160]{3,1,2,0:T(1,128)} fusion(f32[8,9,129,160]{3,2,1,0:T(8,128)S(1)} %get-tuple-element.53, pred[8,9,1,1]{1,0,2,3:T(8,128)(4,1)S(1)} %get-tuple-element.71), kind=kOutput, calls=%fused_computation.28 | convolution fusion | flops 17832960 | bytes 6604872 | tf_op jit(solution)/shard_map/is,isfc->ifc/dot_general | solution.py:78
  69.9 9.5 %fusion.58 = f32[8,1,129,160]{3,1,2,0:T(1,128)} fusion(f32[8,9,129,160]{3,2,1,0:T(8,128)S(1)} %get-tuple-element.52, pred[8,9,1,1]{1,0,2,3:T(8,128)(4,1)S(1)} %get-tuple-element.70), kind=kOutput, calls=%fused_computation.58 | convolution fusion | flops 17832960 | bytes 6604872 | tf_op jit(solution)/shard_map/is,isfc->ifc/dot_general | solution.py:77
  79.3 9.9 %fusion.26 = f32[8,1,129,160]{3,1,2,0:T(1,128)} fusion(f32[8,9,129,160]{3,2,1,0:T(8,128)S(1)} %get-tuple-element.53, pred[8,9,1,1]{1,0,2,3:T(8,128)(4,1)S(1)} %get-tuple-element.70), kind=kOutput, calls=%fused_computation.26 | convolution fusion | flops 17832960 | bytes 6604872 | tf_op jit(solution)/shard_map/is,isfc->ifc/dot_general | solution.py:78
  89.2 9.5 %fusion.56 = f32[8,1,129,160]{3,1,2,0:T(1,128)} fusion(f32[8,9,129,160]{3,2,1,0:T(8,128)S(1)} %get-tuple-element.52, pred[8,9,1,1]{1,0,2,3:T(8,128)(4,1)S(1)} %get-tuple-element.69), kind=kOutput, calls=%fused_computation.56 | convolution fusion | flops 17832960 | bytes 6604872 | tf_op jit(solution)/shard_map/is,isfc->ifc/dot_general | solution.py:77
  98.7 9.7 %fusion.24 = f32[8,1,129,160]{3,1,2,0:T(1,128)} fusion(f32[8,9,129,160]{3,2,1,0:T(8,128)S(1)} %get-tuple-element.53, pred[8,9,1,1]{1,0,2,3:T(8,128)(4,1)S(1)} %get-tuple-element.69), kind=kOutput, calls=%fused_computation.24 | convolution fusion | flops 17832960 | bytes 6604872 | tf_op jit(solution)/shard_map/is,isfc->ifc/dot_general | solution.py:78
  108.4 9.5 %fusion.54 = f32[8,1,129,160]{3,1,2,0:T(1,128)} fusion(f32[8,9,129,160]{3,2,1,0:T(8,128)S(1)} %get-tuple-element.52, pred[8,9,1,1]{1,0,2,3:T(8,128)(4,1)S(1)} %get-tuple-element.68), kind=kOutput, calls=%fused_computation.54 | convolution fusion | flops 17832960 | bytes 6604872 | tf_op jit(solution)/shard_map/is,isfc->ifc/dot_general | solution.py:77
  117.9 9.7 %fusion.22 = f32[8,1,129,160]{3,1,2,0:T(1,128)} fusion(f32[8,9,129,160]{3,2,1,0:T(8,128)S(1)} %get-tuple-element.53, pred[8,9,1,1]{1,0,2,3:T(8,128)(4,1)S(1)} %get-tuple-element.68), kind=kOutput, calls=%fused_computation.22 | convolution fusion | flops 17832960 | bytes 6604872 | tf_op jit(solution)/shard_map/is,isfc->ifc/dot_general | solution.py:78
  127.5 9.5 %fusion.52 = f32[8,1,129,160]{3,1,2,0:T(1,128)} fusion(f32[8,9,129,160]{3,2,1,0:T(8,128)S(1)} %get-tuple-element.52, pred[8,9,1,1]{1,0,2,3:T(8,128)(4,1)S(1)} %get-tuple-element.67), kind=kOutput, calls=%fused_computation.52 | convolution fusion | flops 17832960 | bytes 6604872 | tf_op jit(solution)/shard_map/is,isfc->ifc/dot_general | solution.py:77
  137.0 9.9 %fusion.20 = f32[8,1,129,160]{3,1,2,0:T(1,128)} fusion(f32[8,9,129,160]{3,2,1,0:T(8,128)S(1)} %get-tuple-element.53, pred[8,9,1,1]{1,0,2,3:T(8,128)(4,1)S(1)} %get-tuple-element.67), kind=kOutput, calls=%fused_computation.20 | convolution fusion | flops 17832960 | bytes 6604872 | tf_op jit(solution)/shard_map/is,isfc->ifc/dot_general | solution.py:78
  146.9 9.5 %fusion.50 = f32[8,1,129,160]{3,1,2,0:T(1,128)} fusion(f32[8,9,129,160]{3,2,1,0:T(8,128)S(1)} %get-tuple-element.52, pred[8,9,1,1]{1,0,2,3:T(8,128)(4,1)S(1)} %get-tuple-element.66), kind=kOutput, calls=%fused_computation.50 | convolution fusion | flops 17832960 | bytes 6604872 | tf_op jit(solution)/shard_map/is,isfc->ifc/dot_general | solution.py:77
  156.4 9.7 %fusion.18 = f32[8,1,129,160]{3,1,2,0:T(1,128)} fusion(f32[8,9,129,160]{3,2,1,0:T(8,128)S(1)} %get-tuple-element.53, pred[8,9,1,1]{1,0,2,3:T(8,128)(4,1)S(1)} %get-tuple-element.66), kind=kOutput, calls=%fused_computation.18 | convolution fusion | flops 17832960 | bytes 6604872 | tf_op jit(solution)/shard_map/is,isfc->ifc/dot_general | solution.py:78
  166.0 9.5 %fusion.48 = f32[8,1,129,160]{3,1,2,0:T(1,128)} fusion(f32[8,9,129,160]{3,2,1,0:T(8,128)S(1)} %get-tuple-element.52, pred[8,9,1,1]{1,0,2,3:T(8,128)(4,1)S(1)} %get-tuple-element.65), kind=kOutput, calls=%fused_computation.48 | convolution fusion | flops 17832960 | bytes 6604872 | tf_op jit(solution)/shard_map/is,isfc->ifc/dot_general | solution.py:77
  175.5 9.7 %fusion.16 = f32[8,1,129,160]{3,1,2,0:T(1,128)} fusion(f32[8,9,129,160]{3,2,1,0:T(8,128)S(1)} %get-tuple-element.53, pred[8,9,1,1]{1,0,2,3:T(8,128)(4,1)S(1)} %get-tuple-element.65), kind=kOutput, calls=%fused_computation.16 | convolution fusion | flops 17832960 | bytes 6604872 | tf_op jit(solution)/shard_map/is,isfc->ifc/dot_general | solution.py:78
  185.2 9.5 %fusion.46 = f32[8,1,129,160]{3,1,2,0:T(1,128)} fusion(f32[8,9,129,160]{3,2,1,0:T(8,128)S(1)} %get-tuple-element.52, pred[8,9,1,1]{1,0,2,3:T(8,128)(4,1)S(1)} %get-tuple-element.64), kind=kOutput, calls=%fused_computation.46 | convolution fusion | flops 17832960 | bytes 6604872 | tf_op jit(solution)/shard_map/is,isfc->ifc/dot_general | solution.py:77
  194.7 9.9 %fusion.14 = f32[8,1,129,160]{3,1,2,0:T(1,128)} fusion(f32[8,9,129,160]{3,2,1,0:T(8,128)S(1)} %get-tuple-element.53, pred[8,9,1,1]{1,0,2,3:T(8,128)(4,1)S(1)} %get-tuple-element.64), kind=kOutput, calls=%fused_computation.14 | convolution fusion | flops 17832960 | bytes 6604872 | tf_op jit(solution)/shard_map/is,isfc->ifc/dot_general | solution.py:78
  204.6 9.5 %fusion.44 = f32[8,1,129,160]{3,1,2,0:T(1,128)} fusion(f32[8,9,129,160]{3,2,1,0:T(8,128)S(1)} %get-tuple-element.52, pred[8,9,1,1]{1,0,2,3:T(8,128)(4,1)S(1)} %get-tuple-element.63), kind=kOutput, calls=%fused_computation.44 | convolution fusion | flops 17832960 | bytes 6604872 | tf_op jit(solution)/shard_map/is,isfc->ifc/dot_general | solution.py:77
  214.1 9.6 %fusion.12 = f32[8,1,129,160]{3,1,2,0:T(1,128)} fusion(f32[8,9,129,160]{3,2,1,0:T(8,128)S(1)} %get-tuple-element.53, pred[8,9,1,1]{1,0,2,3:T(8,128)(4,1)S(1)} %get-tuple-element.63), kind=kOutput, calls=%fused_computation.12 | convolution fusion | flops 17832960 | bytes 6604872 | tf_op jit(solution)/shard_map/is,isfc->ifc/dot_general | solution.py:78
  223.7 9.5 %fusion.42 = f32[8,1,129,160]{3,1,2,0:T(1,128)} fusion(f32[8,9,129,160]{3,2,1,0:T(8,128)S(1)} %get-tuple-element.52, pred[8,9,1,1]{1,0,2,3:T(8,128)(4,1)S(1)} %copy-done.15), kind=kOutput, calls=%fused_computation.42 | convolution fusion | flops 17832960 | bytes 6604872 | tf_op jit(solution)/shard_map/is,isfc->ifc/dot_general | solution.py:77
  233.2 9.7 %fusion.10 = f32[8,1,129,160]{3,1,2,0:T(1,128)} fusion(f32[8,9,129,160]{3,2,1,0:T(8,128)S(1)} %get-tuple-element.53, pred[8,9,1,1]{1,0,2,3:T(8,128)(4,1)S(1)} %copy-done.15), kind=kOutput, calls=%fused_computation.10 | convolution fusion | flops 17832960 | bytes 6604872 | tf_op jit(solution)/shard_map/is,isfc->ifc/dot_general | solution.py:78
  242.9 9.5 %fusion.40 = f32[8,1,129,160]{3,1,2,0:T(1,128)} fusion(f32[8,9,129,160]{3,2,1,0:T(8,128)S(1)} %get-tuple-element.52, pred[8,9,1,1]{1,0,2,3:T(8,128)(4,1)S(1)} %copy-done.14), kind=kOutput, calls=%fused_computation.40 | convolution fusion | flops 17832960 | bytes 6604872 | tf_op jit(solution)/shard_map/is,isfc->ifc/dot_general | solution.py:77
  252.4 9.9 %fusion.8 = f32[8,1,129,160]{3,1,2,0:T(1,128)} fusion(f32[8,9,129,160]{3,2,1,0:T(8,128)S(1)} %get-tuple-element.53, pred[8,9,1,1]{1,0,2,3:T(8,128)(4,1)S(1)} %copy-done.14), kind=kOutput, calls=%fused_computation.8 | convolution fusion | flops 17832960 | bytes 6604872 | tf_op jit(solution)/shard_map/is,isfc->ifc/dot_general | solution.py:78
  262.3 9.5 %fusion.38 = f32[8,1,129,160]{3,1,2,0:T(1,128)} fusion(f32[8,9,129,160]{3,2,1,0:T(8,128)S(1)} %get-tuple-element.52, pred[8,9,1,1]{1,0,2,3:T(8,128)(4,1)S(1)} %copy-done.13), kind=kOutput, calls=%fused_computation.38 | convolution fusion | flops 17832960 | bytes 6604872 | tf_op jit(solution)/shard_map/is,isfc->ifc/dot_general | solution.py:77
  271.8 9.6 %fusion.6 = f32[8,1,129,160]{3,1,2,0:T(1,128)} fusion(f32[8,9,129,160]{3,2,1,0:T(8,128)S(1)} %get-tuple-element.53, pred[8,9,1,1]{1,0,2,3:T(8,128)(4,1)S(1)} %copy-done.13), kind=kOutput, calls=%fused_computation.6 | convolution fusion | flops 17832960 | bytes 6604872 | tf_op jit(solution)/shard_map/is,isfc->ifc/dot_general | solution.py:78
  281.4 9.5 %fusion.36 = f32[8,1,129,160]{3,1,2,0:T(1,128)} fusion(f32[8,9,129,160]{3,2,1,0:T(8,128)S(1)} %get-tuple-element.52, pred[8,9,1,1]{1,0,2,3:T(8,128)(4,1)S(1)} %copy-done.12), kind=kOutput, calls=%fused_computation.36 | convolution fusion | flops 17832960 | bytes 6604872 | tf_op jit(solution)/shard_map/is,isfc->ifc/dot_general | solution.py:77
  290.9 9.7 %fusion.4 = f32[8,1,129,160]{3,1,2,0:T(1,128)} fusion(f32[8,9,129,160]{3,2,1,0:T(8,128)S(1)} %get-tuple-element.53, pred[8,9,1,1]{1,0,2,3:T(8,128)(4,1)S(1)} %copy-done.12), kind=kOutput, calls=%fused_computation.4 | convolution fusion | flops 17832960 | bytes 6604872 | tf_op jit(solution)/shard_map/is,isfc->ifc/dot_general | solution.py:78
  300.6 9.5 %fusion.34 = f32[8,1,129,160]{3,1,2,0:T(1,128)} fusion(f32[8,9,129,160]{3,2,1,0:T(8,128)S(1)} %get-tuple-element.52, pred[8,9,1,1]{1,0,2,3:T(8,128)(4,1)S(1)} %copy-done.11), kind=kOutput, calls=%fused_computation.34 | convolution fusion | flops 17832960 | bytes 6604872 | tf_op jit(solution)/shard_map/is,isfc->ifc/dot_general | solution.py:77
  310.1 9.8 %fusion.2 = f32[8,1,129,160]{3,1,2,0:T(1,128)} fusion(f32[8,9,129,160]{3,2,1,0:T(8,128)S(1)} %get-tuple-element.53, pred[8,9,1,1]{1,0,2,3:T(8,128)(4,1)S(1)} %copy-done.11), kind=kOutput, calls=%fused_computation.2 | convolution fusion | flops 17832960 | bytes 6604872 | tf_op jit(solution)/shard_map/is,isfc->ifc/dot_general | solution.py:78
  326.7 8.2 %copy.28 = bf16[4,8,64,4,160]{4,2,3,1,0:T(8,128)(2,1)} copy(bf16[4,8,64,4,160]{2,1,0,4,3:T(8,128)(2,1)} %bitcast.198) | data formatting | bytes 5242880 | tf_op jit(solution)/shard_map/all_to_all | solution.py:60
  347.8 12.5 %fusion = f32[8,1,129,160]{3,1,2,0:T(1,128)} fusion(f32[8,9,129,160]{3,2,1,0:T(8,128)} %copy-done.2, pred[8,9,1,1]{1,0,2,3:T(8,128)(4,1)S(1)} %copy-done.10), kind=kOutput, calls=%fused_computation | convolution fusion | flops 17832960 | bytes 6604872 | tf_op jit(solution)/shard_map/is,isfc->ifc/dot_general | solution.py:78
  475.4 12.2 %fusion.32 = f32[8,1,129,160]{3,1,2,0:T(1,128)} fusion(f32[8,9,129,160]{3,2,1,0:T(8,128)} %copy-done.1, pred[8,9,1,1]{1,0,2,3:T(8,128)(4,1)S(1)} %copy-done.10), kind=kOutput, calls=%fused_computation.32 | convolution fusion | flops 17832960 | bytes 6604872 | tf_op jit(solution)/shard_map/is,isfc->ifc/dot_general | solution.py:77
  492.0 11.0 %fusion.86 = f32[258,4,16,160]{0,3,2,1:T(8,128)} fusion(bf16[4,4,256,160]{2,3,1,0:T(8,128)(2,1)} %collective-permute-done.1, bf16[4,8,256,160]{2,3,1,0:T(8,128)(2,1)} %copy.29, bf16[4,4,256,160]{2,3,1,0:T(8,128)(2,1)} %collective-permute-done, f32[256,129]{0,1:T(8,128)S(1)} %copy-done.6, f32[256,129]{0,1:T(8,128)S(1)} %copy-done.8), kind=kOutput, calls=%fused_computation.109 | convolution fusion | flops 1368721920 | bytes 16074752 | tf_op jit(solution)/shard_map/ejlc,lg->ejgc/dot_general | solution.py:46
  503.0 11.1 %add_bitcast_fusion = f32[4,16,258,160]{2,3,1,0:T(8,128)} fusion(f32[258,4,16,160]{0,3,2,1:T(8,128)} %fusion.86, bf16[4,4,256,160]{2,3,1,0:T(8,128)(2,1)} %collective-permute-done.1, bf16[4,8,256,160]{2,3,1,0:T(8,128)(2,1)S(1)} %copy-done.3, bf16[4,4,256,160]{2,3,1,0:T(8,128)(2,1)} %collective-permute-done, f32[256,129]{0,1:T(8,128)S(1)} %copy-done.6, ...), kind=kOutput, calls=%fused_computation.65 | convolution fusion | flops 1371297792 | bytes 26642432 | tf_op jit(solution)/shard_map/ejlc,lg->ejgc/dot_general | solution.py:45
  514.1 10.9 %slice_bitcast_fusion.31 = (f32[4,129,160]{1,2,0:T(8,128)}, f32[4,129,160]{1,2,0:T(8,128)}, f32[4,129,160]{1,2,0:T(8,128)}, f32[4,129,160]{1,2,0:T(8,128)}, f32[...) fusion(f32[4,16,258,160]{2,3,1,0:T(8,128)} %add_bitcast_fusion), kind=kLoop, calls=%fused_computation.146 | loop fusion | bytes 12549120 | tf_op jit(solution)/shard_map/mul | solution.py:81
  525.0 8.1 %slice_bitcast_fusion.30 = (f32[4,129,160]{1,2,0:T(8,128)}, f32[4,129,160]{1,2,0:T(8,128)}, f32[4,129,160]{1,2,0:T(8,128)}, f32[4,129,160]{1,2,0:T(8,128)}, f32[...) fusion(f32[4,16,258,160]{2,3,1,0:T(8,128)} %add_bitcast_fusion), kind=kLoop, calls=%fused_computation.145 | loop fusion | bytes 8586240 | tf_op jit(solution)/shard_map/mul | solution.py:81
  533.2 28.3 %multiply_subtract_fusion = f32[4,8,129,160]{2,3,1,0:T(8,128)} fusion(f32[4,129,160]{1,2,0:T(8,128)} %get-tuple-element.8, f32[8,129,160]{1,2,0:T(8,128)S(1)} %bitcast.201, f32[4,129,160]{1,2,0:T(8,128)} %get-tuple-element.9, f32[8,129,160]{1,2,0:T(8,128)} %bitcast.263, f32[4,129,160]{1,2,0:T(8,128)} %get-tuple-element.10, f32[8,129,160]{1,2,0:T(8,128)} %bitcast.261, ...), kind=kLoop, calls=%fused_computation.99 | loop fusion | flops 41610240 | bytes 34344960 | tf_op jit(solution)/shard_map/sub | solution.py:81
  561.5 28.5 %multiply_add_fusion.2 = f32[4,8,129,160]{2,3,1,0:T(8,128)} fusion(f32[4,129,160]{1,2,0:T(8,128)} %get-tuple-element.8, f32[8,129,160]{1,2,0:T(8,128)S(1)} %bitcast.202, f32[4,129,160]{1,2,0:T(8,128)} %get-tuple-element.9, f32[8,129,160]{1,2,0:T(8,128)} %bitcast.264, f32[4,129,160]{1,2,0:T(8,128)} %get-tuple-element.10, f32[8,129,160]{1,2,0:T(8,128)} %bitcast.262, ...), kind=kLoop, calls=%fused_computation.98 | loop fusion | flops 41610240 | bytes 34344960 | tf_op jit(solution)/shard_map/add | solution.py:82
  590.0 12.6 %convert_bitcast_fusion.1 = bf16[4,8,256,160]{2,3,1,0:T(8,128)(2,1)} fusion(f32[4,8,129,160]{2,3,1,0:T(8,128)} %multiply_add_fusion.2, f32[4,8,129,160]{2,3,1,0:T(8,128)} %multiply_subtract_fusion, f32[129,256]{1,0:T(8,128)S(1)} %get-tuple-element.55, f32[129,256]{1,0:T(8,128)S(1)} %get-tuple-element.54), kind=kOutput, calls=%fused_computation.106 | convolution fusion | flops 4060752896 | bytes 8169472 | tf_op jit(solution)/shard_map/eigc,gl->eilc/dot_general | solution.py:84
  602.6 7.6 copy.32
  610.2 97.3 %all_to_all.27 = bf16[4,8,256,160]{3,1,0,2:T(8,128)(2,1)S(1)} all-to-all(bf16[4,8,256,160]{3,1,0,2:T(8,128)(2,1)} %copy.32), channel_id=1, replica_groups=mesh['lat'=8,'lon'=4] {'lon'}, dimensions={2} | all-to-all | bytes 5242880 | tf_op jit(solution)/shard_map/all_to_all | solution.py:87
  715.8 13.8 %copy.34 = f32[4,8,64,4,160]{4,3,2,1,0:T(4,128)} copy(f32[4,8,64,4,160]{4,2,3,1,0:T(8,128)} %get-tuple-element.40) | data formatting | bytes 10485760 | tf_op jit(solution)/shard_map/convert_element_type | solution.py:87
  729.6 9.6 %reshape.71 = f32[4,8,64,640]{3,2,1,0:T(8,128)} reshape(f32[4,8,64,4,160]{4,3,2,1,0:T(4,128)} %copy.34) | data formatting | bytes 10485760 | tf_op jit(solution)/shard_map/convert_element_type | solution.py:87
  739.3 8.7 %fusion.85 = (u8[4,64,1280]{2,1,0:T(8,128)(4,1)S(1)}, u8[4,64,1280]{2,1,0:T(8,128)(4,1)S(1)}, f32[4,8,64,1280]{3,2,1,0:T(8,128)S(1)}) fusion(f32[1280]{0:T(1024)S(1)} %copy-done.19, bf16[640,1280]{1,0:T(8,128)(2,1)S(1)} %copy-done, f32[4,8,64,640]{3,2,1,0:T(8,128)} %reshape.71, f32[640]{0:T(1024)S(1)} %copy-done.20, f32[4,8,64]{2,1,0:T(8,128)S(1)} %add_rsqrt_fusion, ...), kind=kOutput, calls=%fused_computation.108 | convolution fusion | flops 3396730880 | bytes 18046464 | tf_op jit(solution)/shard_map/eblc,ch->eblh/dot_general | solution.py:94
  748.0 27.9 %add_convert_fusion = bf16[4,8,64,640]{3,2,1,0:T(8,128)(2,1)} fusion(bf16[4,8,64,640]{3,2,1,0:T(8,128)(2,1)S(1)} %copy-done.4, f32[4,8,64,1280]{3,2,1,0:T(8,128)S(1)} %get-tuple-element.72, f32[1280]{0:T(1024)S(1)} %copy-done.19, bf16[1280,640]{1,0:T(8,128)(2,1)S(1)} %copy-done.18, u8[4,64,1280]{2,1,0:T(8,128)(4,1)S(1)} %get-tuple-element.6, ...), kind=kOutput, calls=%fused_computation.96 | convolution fusion | flops 3545497600 | bytes 18027520 | tf_op jit(solution)/shard_map/eblh,hc->eblc/dot_general | solution.py:97
  (99 shorter events, 161.8 us)
Async XLA Ops:
  0.0 739.3 %copy-start = (bf16[640,1280]{1,0:T(8,128)(2,1)S(1)}, bf16[640,1280]{1,0:T(8,128)(2,1)}, u32[]{:S(2)}) copy-start(bf16[640,1280]{1,0:T(8,128)(2,1)} %param.15) | copy-start | bytes 4915204
  9.0 12.7 %copy-start.9 = (f32[8,9,3,256]{3,0,2,1:T(8,128)S(1)}, f32[8,9,3,256]{3,0,2,1:T(8,128)}, u32[]{:S(2)}) copy-start(f32[8,9,3,256]{3,0,2,1:T(8,128)} %param.10) | copy-start | bytes 663556
  15.9 6.9 copy-start.16
  15.9 6.9 copy-start.21
  15.9 6.9 copy-start.17
  15.9 304.0 %all-to-all-start = ((bf16[4,2,163840]{2,1,0:T(2,128)(2,1)}), bf16[4,2,163840]{2,1,0:T(2,128)(2,1)}, u32[]{:S(2)}, u32[]{:S(2)}) async-start(bf16[4,2,163840]{2,1,0:T(2,128)(2,1)} %reshape.128), calls=%async_computation | async-start | bytes 5242880 | tf_op jit(solution)/shard_map/all_to_all | solution.py:60
  21.7 1.0 copy-start.5
  21.7 1.0 copy-start.7
  31.5 269.1 %copy-start.1 = (f32[8,9,129,160]{3,2,1,0:T(8,128)}, f32[8,9,129,160]{3,2,1,0:T(8,128)S(1)}, u32[]{:S(2)}) copy-start(f32[8,9,129,160]{3,2,1,0:T(8,128)S(1)} %get-tuple-element.52) | copy-start | bytes 17832964
  31.5 278.6 %copy-start.2 = (f32[8,9,129,160]{3,2,1,0:T(8,128)}, f32[8,9,129,160]{3,2,1,0:T(8,128)S(1)}, u32[]{:S(2)}) copy-start(f32[8,9,129,160]{3,2,1,0:T(8,128)S(1)} %get-tuple-element.53) | copy-start | bytes 17832964
  214.1 9.6 %copy-start.15 = (pred[8,9,1,1]{1,0,2,3:T(8,128)(4,1)S(1)}, pred[8,9,1,1]{1,0,2,3:T(8,128)(4,1)}, u32[]{:S(2)}) copy-start(pred[8,9,1,1]{1,0,2,3:T(8,128)(4,1)} %get-tuple-element.62) | copy-start | bytes 220
  233.2 9.7 %copy-start.14 = (pred[8,9,1,1]{1,0,2,3:T(8,128)(4,1)S(1)}, pred[8,9,1,1]{1,0,2,3:T(8,128)(4,1)}, u32[]{:S(2)}) copy-start(pred[8,9,1,1]{1,0,2,3:T(8,128)(4,1)} %get-tuple-element.61) | copy-start | bytes 220
  252.4 9.9 %copy-start.13 = (pred[8,9,1,1]{1,0,2,3:T(8,128)(4,1)S(1)}, pred[8,9,1,1]{1,0,2,3:T(8,128)(4,1)}, u32[]{:S(2)}) copy-start(pred[8,9,1,1]{1,0,2,3:T(8,128)(4,1)} %get-tuple-element.60) | copy-start | bytes 220
  271.8 9.6 %copy-start.12 = (pred[8,9,1,1]{1,0,2,3:T(8,128)(4,1)S(1)}, pred[8,9,1,1]{1,0,2,3:T(8,128)(4,1)}, u32[]{:S(2)}) copy-start(pred[8,9,1,1]{1,0,2,3:T(8,128)(4,1)} %get-tuple-element.59) | copy-start | bytes 220
  290.9 9.7 %copy-start.11 = (pred[8,9,1,1]{1,0,2,3:T(8,128)(4,1)S(1)}, pred[8,9,1,1]{1,0,2,3:T(8,128)(4,1)}, u32[]{:S(2)}) copy-start(pred[8,9,1,1]{1,0,2,3:T(8,128)(4,1)} %get-tuple-element.58) | copy-start | bytes 220
  334.9 13.0 %copy-start.10 = (pred[8,9,1,1]{1,0,2,3:T(8,128)(4,1)S(1)}, pred[8,9,1,1]{1,0,2,3:T(8,128)(4,1)}, u32[]{:S(2)}) copy-start(pred[8,9,1,1]{1,0,2,3:T(8,128)(4,1)} %get-tuple-element.57) | copy-start | bytes 220
  344.2 147.8 %collective-permute-start = (bf16[4,4,256,160]{2,3,1,0:T(8,128)(2,1)}, bf16[4,4,256,160]{2,3,1,0:T(8,128)(2,1)}, u32[]{:S(2)}, u32[]{:S(2)}) collective-permute-start(bf16[4,4,256,160]{2,3,1,0:T(8,128)(2,1)} %get-tuple-element.41), channel_id=1, source_target_pairs={{0,4},{4,8},{8,12},{12,16},{16,20},{20,24},{24,28},{1,5},{5,9},{9,... | collective-permute-start | bytes 3932168 | tf_op jit(solution)/shard_map/ppermute | solution.py:19
  346.5 145.4 %collective-permute-start.1 = (bf16[4,4,256,160]{2,3,1,0:T(8,128)(2,1)}, bf16[4,4,256,160]{2,3,1,0:T(8,128)(2,1)}, u32[]{:S(2)}, u32[]{:S(2)}) collective-permute-start(bf16[4,4,256,160]{2,3,1,0:T(8,128)(2,1)} %get-tuple-element.42), channel_id=1, source_target_pairs={{4,0},{8,4},{12,8},{16,12},{20,16},{24,20},{28,24},{5,1},{9,5},{13... | collective-permute-start | bytes 3932168 | tf_op jit(solution)/shard_map/ppermute | solution.py:20
  475.4 16.6 %copy-start.6 = (f32[256,129]{0,1:T(8,128)S(1)}, f32[256,129]{0,1:T(8,128)}, u32[]{:S(2)}) copy-start(f32[256,129]{0,1:T(8,128)} %copy-done.5) | copy-start | bytes 396292
  475.4 16.6 %copy-start.8 = (f32[256,129]{0,1:T(8,128)S(1)}, f32[256,129]{0,1:T(8,128)}, u32[]{:S(2)}) copy-start(f32[256,129]{0,1:T(8,128)} %copy-done.7) | copy-start | bytes 396292
  491.9 11.1 %copy-start.3 = (bf16[4,8,256,160]{2,3,1,0:T(8,128)(2,1)S(1)}, bf16[4,8,256,160]{2,3,1,0:T(8,128)(2,1)}, u32[]{:S(2)}) copy-start(bf16[4,8,256,160]{2,3,1,0:T(8,128)(2,1)} %copy.29) | copy-start | bytes 7864324
  729.6 9.6 %copy-start.19 = (f32[1280]{0:T(1024)S(1)}, f32[1280]{0:T(1024)}, u32[]{:S(2)}) copy-start(f32[1280]{0:T(1024)} %param.16) | copy-start | bytes 15364
  729.6 9.6 %copy-start.20 = (f32[640]{0:T(1024)S(1)}, f32[640]{0:T(1024)}, u32[]{:S(2)}) copy-start(f32[640]{0:T(1024)} %param.14) | copy-start | bytes 7684
  739.3 8.7 %copy-start.4 = (bf16[4,8,64,640]{3,2,1,0:T(8,128)(2,1)S(1)}, bf16[4,8,64,640]{3,2,1,0:T(8,128)(2,1)}, u32[]{:S(2)}) copy-start(bf16[4,8,64,640]{3,2,1,0:T(8,128)(2,1)} %param.9) | copy-start | bytes 7864324
  739.3 8.7 %copy-start.18 = (bf16[1280,640]{1,0:T(8,128)(2,1)S(1)}, bf16[1280,640]{1,0:T(8,128)(2,1)}, u32[]{:S(2)}) copy-start(bf16[1280,640]{1,0:T(8,128)(2,1)} %param.17) | copy-start | bytes 4915204
where the time goes:
time: 790 us; the launch traced here: 776 us
  matrix products  385 us (49%)
  local copies, waits for them, and re-layouts  209 us (26%)
  blocking collectives  97.3 us (12%)
  other arithmetic  75 us (9%)
  starting transfers between devices  8.88 us (1%)
    dot_general x16, matrix products, shards(): jnp.einsum('is,isfc->ifc', select, mixed_im, precision=lax.Precision.HIGH...  159 us
    dot_general x16, matrix products, shards(): jnp.einsum('is,isfc->ifc', select, mixed_re, precision=lax.Precision.HIGH...  155 us
    all_to_all x1, blocking collectives, shards(): lax.all_to_all(conv, 'lon', split_axis=2, concat_axis=3, tiled=True)  97.3 us
    dot_general x16, local copies, waits for them, and re-layouts, shards(): jnp.einsum('is,isfc->ifc', select, mixed_re, precision=lax.Precision.HIGH...  60 us
    dot_general x16, local copies, waits for them, and re-layouts, shards(): jnp.einsum('is,isfc->ifc', select, mixed_im, precision=lax.Precision.HIGH...  58.7 us
    add x1, other arithmetic, shards(): total_im = total_im + coef_re * row_im + coef_im * row_re  28.5 us
    sub x1, other arithmetic, shards(): total_re = total_re + coef_re * row_re - coef_im * row_im  28.3 us
    dot_general x1, matrix products, shards(): jnp.einsum('eblh,hc->eblc', hidden, w_out, preferred_element_type=jnp.flo...  27.9 us
  transfers between devices with their start and end apart: 3, of which 0 were waited for; matrix products, arithmetic and copies ran while one was open for 57% of the time, Pallas kernels for 0%

commit v1 on v0

--- a/solution.py
+++ b/solution.py
@@ -1,12 +1,278 @@
+import functools
 import math
 
 import jax
 import jax.numpy as jnp
 from jax import lax
+from jax.experimental import pallas as pl
+from jax.experimental.pallas import tpu as pltpu
 from jax.sharding import PartitionSpec as P
 
 REACH = 4
-SLOTS = 9
+WINDOW = 2 * REACH + 1
+LANES = 128
+MESH = pl.DeviceIdType.MESH
+
+
+def windowed(kernel, row_start, row_count, first):
+    rows, slots = kernel.shape[:2]
+    centre = first + jnp.arange(rows, dtype=jnp.int32)
+    shift = row_start - (centre - REACH)
+    place = jnp.arange(WINDOW, dtype=jnp.int32)[None, :] - shift[:, None]
+    total = jnp.zeros((rows, WINDOW) + kernel.shape[2:], jnp.float32)
+    for slot in range(slots):
+        hit = (place == slot) & (slot < row_count[:, None])
+        total = total + jnp.where(hit[:, :, None, None], kernel[:, slot][:, None], 0.0)
+    return jnp.roll(total[..., ::-1], 1, axis=-1)
+
+
+def gather_kernel(
+    L, T, members, fields, theta, taps, wide_out, base_out, theta_out,
+    wide, build, theta_buf, send_sem, recv_sem, halo_send, halo_recv, th_send, th_recv, local_sem, out_sem, build_sem,
+):
+    lat, lon = lax.axis_index("lat"), lax.axis_index("lon")
+    up, down = lax.rem(lat + 1, T), lax.rem(lat + T - 1, T)
+    rows, cols = fields.shape[1], fields.shape[2]
+    circle = wide.shape[2]
+    basis = taps.shape[1] // WINDOW
+
+    barrier = pltpu.get_barrier_semaphore()
+    for step in range(1, L):
+        pl.semaphore_signal(barrier, inc=1, device_id={"lon": lax.rem(lon + step, L)}, device_id_type=MESH)
+    for other in (up, down):
+        pl.semaphore_signal(barrier, inc=1, device_id={"lat": other}, device_id_type=MESH)
+    pl.semaphore_wait(barrier, L + 1)
+
+    def slab(owner):
+        return wide.at[:, pl.ds(REACH, rows), pl.ds(pl.multiple_of(owner * cols, cols), cols), :]
+
+    sends = []
+    for step in range(1, L):
+        peer = lax.rem(lon + step, L)
+        sends.append(pltpu.make_async_remote_copy(
+            src_ref=fields.at[pl.ds(peer * members, members)], dst_ref=slab(lon),
+            send_sem=send_sem.at[step], recv_sem=recv_sem.at[step],
+            device_id={"lon": peer}, device_id_type=MESH))
+        sends.append(pltpu.make_async_remote_copy(
+            src_ref=theta, dst_ref=theta_buf.at[lon],
+            send_sem=th_send.at[step], recv_sem=th_recv.at[step],
+            device_id={"lon": peer}, device_id_type=MESH))
+    for copy in sends:
+        copy.start()
+    mine = pltpu.make_async_copy(fields.at[pl.ds(lon * members, members)], slab(lon), local_sem.at[0])
+    mine_theta = pltpu.make_async_copy(theta, theta_buf.at[lon], local_sem.at[1])
+    mine.start()
+    mine_theta.start()
+    mine.wait()
+    mine_theta.wait()
+
+    def forward(step, owner):
+        part = pl.ds(pl.multiple_of(owner * cols, cols), cols)
+        low = pltpu.make_async_remote_copy(
+            src_ref=wide.at[:, pl.ds(REACH, REACH), part, :],
+            dst_ref=wide.at[:, pl.ds(REACH + rows, REACH), part, :],
+            send_sem=halo_send.at[0, step], recv_sem=halo_recv.at[0, step],
+            device_id={"lat": down}, device_id_type=MESH)
+        high = pltpu.make_async_remote_copy(
+            src_ref=wide.at[:, pl.ds(rows, REACH), part, :],
+            dst_ref=wide.at[:, pl.ds(0, REACH), part, :],
+            send_sem=halo_send.at[1, step], recv_sem=halo_recv.at[1, step],
+            device_id={"lat": up}, device_id_type=MESH)
+        low.start()
+        high.start()
+        return [low, high]
+
+    halos = forward(0, lon)
+
+    def build_row(i, carry):
+        slot = lax.rem(i, 2)
+        out = pltpu.make_async_copy(build.at[slot], base_out.at[i], build_sem.at[slot])
+
+        @pl.when(i >= 2)
+        def _():
+            out.wait()
+
+        for w in range(WINDOW):
+            for k in range(basis):
+                line = taps[i, pl.ds(w * basis + k, 1), :]
+                block = pltpu.roll(jnp.broadcast_to(line, (LANES, circle)), 0, 1, stride=1, stride_axis=0)
+                build[slot, pl.ds(k * LANES, LANES), pl.ds(w * circle, circle)] = block.astype(jnp.bfloat16)
+        out.start()
+        return carry
+
+    lax.fori_loop(0, rows, build_row, 0)
+    for slot in range(2):
+        pltpu.make_async_copy(build.at[slot], base_out.at[slot], build_sem.at[slot]).wait()
+
+    for step in range(1, L):
+        owner = lax.rem(lon + L - step, L)
+        sends[2 * (step - 1)].wait_recv()
+        sends[2 * (step - 1) + 1].wait_recv()
+        halos += forward(step, owner)
+    theta_copy = pltpu.make_async_copy(theta_buf, theta_out, local_sem.at[1])
+    theta_copy.start()
+    for copy in halos:
+        copy.wait_recv()
+    whole = pltpu.make_async_copy(wide, wide_out, out_sem)
+    whole.start()
+    for copy in sends + halos:
+        copy.wait_send()
+    theta_copy.wait()
+    whole.wait()
+
+
+def gather(fields, theta, taps, L, T):
+    ens, rows, cols, chans = fields.shape
+    members, circle = ens // L, cols * L
+    basis = taps.shape[1] // WINDOW
+    span = rows + 2 * REACH
+    any_space = pl.BlockSpec(memory_space=pl.ANY)
+    vmem = pl.BlockSpec(memory_space=pltpu.VMEM)
+    wide = (members, span, circle, chans)
+    base = (rows, basis * LANES, WINDOW * circle)
+    dma = pltpu.SemaphoreType.DMA
+    return pl.pallas_call(
+        functools.partial(gather_kernel, L, T, members),
+        out_shape=(
+            jax.ShapeDtypeStruct(wide, jnp.bfloat16),
+            jax.ShapeDtypeStruct(base, jnp.bfloat16),
+            jax.ShapeDtypeStruct((L,) + theta.shape, jnp.float32),
+        ),
+        in_specs=[any_space, vmem, vmem],
+        out_specs=(any_space, any_space, any_space),
+        scratch_shapes=[
+            pltpu.VMEM(wide, jnp.bfloat16),
+            pltpu.VMEM((2,) + base[1:], jnp.bfloat16),
+            pltpu.VMEM((L,) + theta.shape, jnp.float32),
+            dma((L,)), dma((L,)), dma((2, L)), dma((2, L)), dma((L,)), dma((L,)), dma((2,)), dma, dma((2,)),
+        ],
+        compiler_params=pltpu.CompilerParams(
+            collective_id=0, has_side_effects=True, vmem_limit_bytes=40 * 2**20),
+        name="gather",
+    )(fields, theta, taps)
+
+
+def conv_kernel(base, wide, theta, out):
+    row = pl.program_id(1)
+    circle, chans = wide.shape[2], wide.shape[3]
+    lhs = base[0]
+    for h in range(circle // LANES):
+        cut = h * LANES
+        pieces = []
+        for w in range(WINDOW):
+            pieces.append(wide[0, row + w, pl.ds(cut, circle - cut), :])
+            if cut:
+                pieces.append(wide[0, row + w, pl.ds(0, cut), :])
+        rhs = jnp.concatenate(pieces, axis=0)
+        prod = jnp.dot(lhs, rhs, preferred_element_type=jnp.float32)
+        total = prod[:LANES] * theta[0:1, :]
+        for k in range(1, theta.shape[0]):
+            total = total + prod[k * LANES:(k + 1) * LANES] * theta[k:k + 1, :]
+        out[0, 0, pl.ds(cut, LANES), :] = total.astype(jnp.bfloat16)
+
+
+def convolve(base, wide, theta):
+    rows = base.shape[0]
+    members, span, circle, chans = wide.shape
+    return pl.pallas_call(
+        conv_kernel,
+        grid=(members, rows),
+        out_shape=jax.ShapeDtypeStruct((members, rows, circle, chans), jnp.bfloat16),
+        in_specs=[
+            pl.BlockSpec((1,) + base.shape[1:], lambda e, i: (i, 0, 0)),
+            pl.BlockSpec((1, span, circle, chans), lambda e, i: (e, 0, 0, 0)),
+            pl.BlockSpec(theta.shape, lambda e, i: (0, 0)),
+        ],
+        out_specs=pl.BlockSpec((1, 1, circle, chans), lambda e, i: (e, i, 0, 0)),
+        compiler_params=pltpu.CompilerParams(vmem_limit_bytes=60 * 2**20),
+        name="convolve",
+    )(base, wide, theta)
+
+
+def mlp_kernel(
+    L, members, tile, conv, fields, gain, w_in, b_in, w_out, out,
+    got, held, res, send_sem, recv_sem, local_sem, out_sem,
+):
+    lon = lax.axis_index("lon")
+    rows, cols, chans = got.shape[1:]
+
+    barrier = pltpu.get_barrier_semaphore()
+    for step in range(1, L):
+        pl.semaphore_signal(barrier, inc=1, device_id={"lon": lax.rem(lon + step, L)}, device_id_type=MESH)
+    pl.semaphore_wait(barrier, L - 1)
+
+    def part(owner):
+        return conv.at[:, :, pl.ds(pl.multiple_of(owner * cols, cols), cols), :]
+
+    sends = []
+    for step in range(1, L):
+        peer = lax.rem(lon + step, L)
+        sends.append(pltpu.make_async_remote_copy(
+            src_ref=part(peer), dst_ref=got.at[pl.ds(lon * members, members)],
+            send_sem=send_sem.at[step], recv_sem=recv_sem.at[step],
+            device_id={"lon": peer}, device_id_type=MESH))
+    for copy in sends:
+        copy.start()
+    mine = pltpu.make_async_copy(part(lon), got.at[pl.ds(lon * members, members)], local_sem.at[0])
+    bring = pltpu.make_async_copy(fields, held, local_sem.at[1])
+    mine.start()
+    bring.start()
+    mine.wait()
+    bring.wait()
+
+    outs = []
+    for step in range(L):
+        owner = lax.rem(lon + L - step, L)
+        if step:
+            sends[step - 1].wait_recv()
+
+        def points(t, carry):
+            member = owner * members + t // (rows // tile)
+            at = pl.ds(lax.rem(t, rows // tile) * tile, tile)
+            values = got[member, at].reshape(tile * cols, chans).astype(jnp.float32)
+            mean = jnp.mean(values, axis=-1, keepdims=True)
+            diff = values - mean
+            var = jnp.mean(diff * diff, axis=-1, keepdims=True)
+            normed = (diff * lax.rsqrt(var + 1e-05) * gain[...]).astype(jnp.bfloat16)
+            hidden = jnp.dot(normed, w_in[...], preferred_element_type=jnp.float32) + b_in[...]
+            hidden = (0.5 * hidden * (1.0 + lax.erf(hidden * math.sqrt(0.5)))).astype(jnp.bfloat16)
+            branch = jnp.dot(hidden, w_out[...], preferred_element_type=jnp.float32)
+            start = held[member, at].reshape(tile * cols, chans).astype(jnp.float32)
+            res[member, at] = (start + branch).astype(jnp.bfloat16).reshape(tile, cols, chans)
+            return carry
+
+        lax.fori_loop(0, members * (rows // tile), points, 0)
+        here = pl.ds(owner * members, members)
+        outs.append(pltpu.make_async_copy(res.at[here], out.at[here], out_sem.at[step]))
+        outs[-1].start()
+    for copy in sends:
+        copy.wait_send()
+    for copy in outs:
+        copy.wait()
+
+
+def mlp(conv, fields, gain, w_in, b_in, w_out, L):
+    ens, rows, cols, chans = fields.shape
+    members = ens // L
+    tile = max(d for d in range(1, rows + 1) if rows % d == 0 and d * cols <= 256)
+    any_space = pl.BlockSpec(memory_space=pl.ANY)
+    vmem = pl.BlockSpec(memory_space=pltpu.VMEM)
+    dma = pltpu.SemaphoreType.DMA
+    return pl.pallas_call(
+        functools.partial(mlp_kernel, L, members, tile),
+        out_shape=jax.ShapeDtypeStruct(fields.shape, jnp.bfloat16),
+        in_specs=[any_space, any_space, vmem, vmem, vmem, vmem],
+        out_specs=any_space,
+        scratch_shapes=[
+            pltpu.VMEM(fields.shape, jnp.bfloat16),
+            pltpu.VMEM(fields.shape, jnp.bfloat16),
+            pltpu.VMEM(fields.shape, jnp.bfloat16),
+            dma((L,)), dma((L,)), dma((2,)), dma((L,)),
+        ],
+        compiler_params=pltpu.CompilerParams(
+            collective_id=1, has_side_effects=True, vmem_limit_bytes=48 * 2**20),
+        name="mlp",
+    )(conv, fields, gain[None, :], w_in, b_in[None, :], w_out)
 
 
 def with_halo(value, sides, width):
@@ -56,7 +322,7 @@
     return mixed
 
 
-def shards(fields, kernel, theta, row_start, row_count, norm_gain, w_in, b_in, w_out):
+def spectral_shards(fields, kernel, theta, row_start, row_count, norm_gain, w_in, b_in, w_out):
     local = lax.all_to_all(fields, "lon", split_axis=3, concat_axis=2, tiled=True)
     members, band, circle, chans = local.shape
     onward, backward, bins = circle_tables(circle)
@@ -67,7 +333,7 @@
     mixed_im = mix_basis(kern_all[..., bins:], theta)
     first_row = lax.axis_index("lat") * band - REACH
     span_rows = band + 2 * REACH
-    slot_ids = jnp.arange(SLOTS, dtype=jnp.int32)
+    slot_ids = jnp.arange(WINDOW, dtype=jnp.int32)
     offsets = row_start - first_row
     live_slot = slot_ids[None, :] < row_count[:, None]
     total_re = jnp.zeros((members, band, bins, chans), jnp.float32)
@@ -98,6 +364,20 @@
     return (fields.astype(jnp.float32) + branch).astype(jnp.bfloat16)
 
 
+def shards(L, T, fields, kernel, theta, row_start, row_count, norm_gain, w_in, b_in, w_out):
+    if fields.shape[0] % L:
+        return spectral_shards(
+            fields, kernel, theta, row_start, row_count, norm_gain, w_in, b_in, w_out
+        )
+    rows = fields.shape[1]
+    taps = windowed(kernel, row_start, row_count, lax.axis_index("lat") * rows)
+    taps = taps.reshape(rows, -1, taps.shape[-1])
+    wide, base, parts = gather(fields, theta, taps, L, T)
+    full = jnp.transpose(parts, (1, 0, 2)).reshape(theta.shape[0], -1)
+    conv = convolve(base, wide, full)
+    return mlp(conv, fields, norm_gain, w_in, b_in, w_out, L)
+
+
 def solution(mesh):
     placed = (
         P(None, "lat", "lon", None),
@@ -111,5 +391,6 @@
         P(),
     )
     return jax.shard_map(
-        shards, mesh=mesh, in_specs=placed, out_specs=P(None, "lat", "lon", None), check_vma=False
-    )
+        functools.partial(shards, mesh.shape["lon"], mesh.shape["lat"]),
+        mesh=mesh, in_specs=placed, out_specs=P(None, "lat", "lon", None), check_vma=False,
+    )

time: 790 us -> 177 us (0.22); the launches traced: 776 us -> 177 us
  matrix products: 385 us -> 0 us
  local copies, waits for them, and re-layouts: 209 us -> 5.96 us
  Pallas kernels: 0 us -> 169 us
  blocking collectives: 97.3 us -> 0 us
  other arithmetic: 75 us -> 1.82 us
  starting transfers between devices: 8.88 us -> 0 us
    dot_general x38 -> x0, matrix products: 385 us -> none  [the longest x16 159 us: shards(): jnp.einsum('is,isfc->ifc', select, mixed_im, precision=lax.Precision.HIGH...]
    pallas_call x0 -> x3, Pallas kernels: none -> 169 us  [the longest x1 75.2 us: gather(): pl.pallas_call(functools.partial(gather_kernel, L, T, members), out_shape...]
    dot_general x32 -> x0, local copies, waits for them, and re-layouts: 119 us -> none  [the longest x16 60 us: shards(): jnp.einsum('is,isfc->ifc', select, mixed_re, precision=lax.Precision.HIGH...]
    all_to_all x1 -> x0, blocking collectives: 97.3 us -> none  [shards(): lax.all_to_all(conv, 'lon', split_axis=2, concat_axis=3, tiled=True)]
    add x2 -> x1, other arithmetic: 36.5 us -> 0.21 us  [windowed(): total + jnp.where(hit[:, :, None, None], kernel[:, slot][:, None], 0.0)]
    convert_element_type x3 -> x0, local copies, waits for them, and re-layouts: 31 us -> none  [the longest x2 23.5 us: shards(): lax.all_to_all(conv, 'lon', split_axis=2, concat_axis=3, tiled=True)]
    sub x2 -> x1, other arithmetic: 28.3 us -> 0.66 us  [windowed(): shift = row_start - (centre - REACH)]
    mul x3 -> x0, local copies, waits for them, and re-layouts: 19.2 us -> none  [the longest x2 19 us: shards(): total_re = total_re + coef_re * row_re - coef_im * row_im]
  transfers between devices with their start and end apart: 3 -> 0, of which waited for: 0 -> 0; matrix products, arithmetic and copies ran while one was open for 57% -> 0% of each run, Pallas kernels for 0% -> 0%
where the time goes in v1:
time: 177 us
  Pallas kernels  169 us (95%)
  local copies, waits for them, and re-layouts  5.96 us (3%)
  other arithmetic  1.82 us (1%)
    pallas_call x1, Pallas kernels, gather(): pl.pallas_call(functools.partial(gather_kernel, L, T, members), out_shape...  75.2 us
    pallas_call x1, Pallas kernels, mlp(): pl.pallas_call(functools.partial(mlp_kernel, L, members, tile), out_shape...  66.8 us
    pallas_call x1, Pallas kernels, convolve(): pl.pallas_call(conv_kernel, grid=(members, rows), out_shape=jax.ShapeDtyp...  27.3 us
    unnamed x17, local copies, waits for them, and re-layouts  4.17 us

profile of v1, /device:TPU:24, one launch (start us, length us, event | category | flops | bytes accessed | tf_op | source)
XLA Modules:
  0.0 177.2 jit_solution(11350841735976491608)
XLA Ops:
  0.0 0.0 copy-start.4
  0.0 0.0 copy-start
  0.0 0.8 broadcast_compare_fusion.8
  0.8 0.7 add_subtract_fusion
  1.5 0.9 slice_bitcast_fusion.8
  2.4 0.2 select_add_fusion
  2.6 0.1 slice.52
  2.7 0.2 reverse.2
  3.0 0.1 slice.62
  3.1 0.1 pad_maximum_fusion
  3.3 0.1 copy.20.taps
  3.3 0.0 copy-done.4
  3.4 0.0 copy-done
  3.4 75.2 %gather.1 = (bf16[1,16,256,640]{3,2,1,0:T(8,128)(2,1)S(1)}, bf16[8,384,2304]{2,1,0:T(8,128)(2,1)}, f32[4,3,160]{2,1,0:T(4,128)S(1)}) custom-call(bf16[4,8,64,640]{3,2,1,0:T(8,128)(2,1)S(1)} %copy-done, f32[3,160]{1,0:T(4,128)S(1)} %copy-done.4, f32[8,27,256]{2,1,0:T(8,128)S(1)} %copy.20.taps), custom_call_target="tpu_custom_call" | custom-call | tf_op jit(solution)/shard_map/gather/pallas_call | solution.py:134
  78.6 0.0 copy-start.1
  78.6 2.3 %copy-done.1 = bf16[1,16,256,640]{3,2,1,0:T(8,128)(2,1)} copy-done((bf16[1,16,256,640]{3,2,1,0:T(8,128)(2,1)}, bf16[1,16,256,640]{3,2,1,0:T(8,128)(2,1)S(1)}, u32[]{:S(2)}) %copy-start.1) | copy-done | bytes 5242904
  80.9 0.7 reshape.326.theta
  81.6 0.0 copy-start.5
  81.6 0.0 copy-start.6
  81.6 0.0 copy-start.2
  81.6 0.0 copy-start.3
  81.6 27.3 %convolve.1.conv = bf16[1,8,256,640]{3,2,1,0:T(8,128)(2,1)} custom-call(bf16[8,384,2304]{2,1,0:T(8,128)(2,1)} %get-tuple-element.8.base, bf16[1,16,256,640]{3,2,1,0:T(8,128)(2,1)} %copy-done.1, f32[3,640]{1,0:T(4,128)} %reshape.326.theta), custom_call_target="tpu_custom_call" | custom-call | tf_op jit(solution)/shard_map/convolve/pallas_call | solution.py:177
  108.9 0.0 copy-done.5
  108.9 0.0 copy-done.6
  108.9 0.0 copy-done.2
  108.9 0.0 copy-done.3
  108.9 66.8 %mlp.1 = bf16[4,8,64,640]{3,2,1,0:T(8,128)(2,1)S(1)} custom-call(bf16[1,8,256,640]{3,2,1,0:T(8,128)(2,1)} %convolve.1.conv, bf16[4,8,64,640]{3,2,1,0:T(8,128)(2,1)} %fields.3, f32[1,640]{1,0:T(1,128)S(1)} %broadcast_in_dim.180.gain, bf16[640,1280]{1,0:T(8,128)(2,1)S(1)} %copy-done.2, f32[1,1280]{1,0:T(1,128)S(1)} %broadcast_in_dim.181.b_in, ...), custom_call_target="tpu_custom_call" | custom-call | tf_op jit(solution)/shard_map/mlp/pallas_call | solution.py:261
  175.7 1.5 copy.23
  (5 shorter events, 0.0 us)
Async XLA Ops:
  0.0 3.3 %copy-start.4 = (f32[3,160]{1,0:T(4,128)S(1)}, f32[3,160]{1,0:T(4,128)}, u32[]{:S(2)}) copy-start(f32[3,160]{1,0:T(4,128)} %theta.1) | copy-start | bytes 5764
  0.0 3.4 %copy-start = (bf16[4,8,64,640]{3,2,1,0:T(8,128)(2,1)S(1)}, bf16[4,8,64,640]{3,2,1,0:T(8,128)(2,1)}, u32[]{:S(2)}) copy-start(bf16[4,8,64,640]{3,2,1,0:T(8,128)(2,1)} %fields.3) | copy-start | bytes 7864324
  78.6 2.3 %copy-start.1 = (bf16[1,16,256,640]{3,2,1,0:T(8,128)(2,1)}, bf16[1,16,256,640]{3,2,1,0:T(8,128)(2,1)S(1)}, u32[]{:S(2)}) copy-start(bf16[1,16,256,640]{3,2,1,0:T(8,128)(2,1)S(1)} %get-tuple-element.9.wide) | copy-start | bytes 15728644
  81.6 27.3 %copy-start.5 = (f32[1280]{0:T(1024)S(1)}, f32[1280]{0:T(1024)}, u32[]{:S(2)}) copy-start(f32[1280]{0:T(1024)} %param.16) | copy-start | bytes 15364
  81.6 27.3 %copy-start.6 = (f32[640]{0:T(1024)S(1)}, f32[640]{0:T(1024)}, u32[]{:S(2)}) copy-start(f32[640]{0:T(1024)} %param.14) | copy-start | bytes 7684
  81.6 27.3 %copy-start.2 = (bf16[640,1280]{1,0:T(8,128)(2,1)S(1)}, bf16[640,1280]{1,0:T(8,128)(2,1)}, u32[]{:S(2)}) copy-start(bf16[640,1280]{1,0:T(8,128)(2,1)} %w_in.1) | copy-start | bytes 4915204
  81.6 27.3 %copy-start.3 = (bf16[1280,640]{1,0:T(8,128)(2,1)S(1)}, bf16[1280,640]{1,0:T(8,128)(2,1)}, u32[]{:S(2)}) copy-start(bf16[1280,640]{1,0:T(8,128)(2,1)} %w_out.1) | copy-start | bytes 4915204

commit v2 on v0

--- a/solution.py
+++ b/solution.py
@@ -1,12 +1,235 @@
+import functools
 import math
 
 import jax
 import jax.numpy as jnp
 from jax import lax
+from jax.experimental import pallas as pl
+from jax.experimental.pallas import tpu as pltpu
 from jax.sharding import PartitionSpec as P
 
 REACH = 4
-SLOTS = 9
+WINDOW = 2 * REACH + 1
+LANES = 128
+MESH = pl.DeviceIdType.MESH
+
+
+def windowed(kernel, row_start, row_count, first):
+    rows, slots = kernel.shape[:2]
+    centre = first + jnp.arange(rows, dtype=jnp.int32)
+    shift = row_start - (centre - REACH)
+    place = jnp.arange(WINDOW, dtype=jnp.int32)[None, :] - shift[:, None]
+    total = jnp.zeros((rows, WINDOW) + kernel.shape[2:], jnp.float32)
+    for slot in range(slots):
+        hit = (place == slot) & (slot < row_count[:, None])
+        total = total + jnp.where(hit[:, :, None, None], kernel[:, slot][:, None], 0.0)
+    return jnp.roll(total[..., ::-1], 1, axis=-1)
+
+
+def block_kernel(
+    L, T, members, fields, theta, taps, gain, w_in, b_in, w_out, out,
+    wide, base, theta_buf, staged, got, held, res,
+    send_sem, recv_sem, halo_send, halo_recv, th_send, th_recv, local_sem, back_send, back_recv, own_sem, out_sem,
+):
+    lat, lon = lax.axis_index("lat"), lax.axis_index("lon")
+    up, down = lax.rem(lat + 1, T), lax.rem(lat + T - 1, T)
+    ens, rows, cols, chans = held.shape
+    circle = wide.shape[2]
+    basis = theta.shape[0]
+
+    bring = pltpu.make_async_copy(fields, held, local_sem.at[2])
+    bring.start()
+    barrier = pltpu.get_barrier_semaphore()
+    for step in range(1, L):
+        pl.semaphore_signal(barrier, inc=1, device_id={"lon": lax.rem(lon + step, L)}, device_id_type=MESH)
+    for other in (up, down):
+        pl.semaphore_signal(barrier, inc=1, device_id={"lat": other}, device_id_type=MESH)
+    pl.semaphore_wait(barrier, L + 1)
+
+    def lons(owner):
+        return pl.ds(pl.multiple_of(owner * cols, cols), cols)
+
+    chunks = [(0, REACH)] + ([(REACH, rows - REACH)] if rows > REACH else [])
+    sends = []
+    for c, (low, size) in enumerate(chunks):
+        row = []
+        for step in range(1, L):
+            peer = lax.rem(lon + step, L)
+            row.append(pltpu.make_async_remote_copy(
+                src_ref=fields.at[pl.ds(peer * members, members), pl.ds(low, size)],
+                dst_ref=wide.at[:, pl.ds(REACH + low, size), lons(lon), :],
+                send_sem=send_sem.at[c, step], recv_sem=recv_sem.at[c, step],
+                device_id={"lon": peer}, device_id_type=MESH))
+            row[-1].start()
+        sends.append(row)
+    shared = []
+    for step in range(1, L):
+        shared.append(pltpu.make_async_remote_copy(
+            src_ref=theta, dst_ref=theta_buf.at[lon],
+            send_sem=th_send.at[step], recv_sem=th_recv.at[step],
+            device_id={"lon": lax.rem(lon + step, L)}, device_id_type=MESH))
+        shared[-1].start()
+    mine = pltpu.make_async_copy(
+        fields.at[pl.ds(lon * members, members)], wide.at[:, pl.ds(REACH, rows), lons(lon), :], local_sem.at[0])
+    mine_theta = pltpu.make_async_copy(theta, theta_buf.at[lon], local_sem.at[1])
+    mine.start()
+    mine_theta.start()
+    mine.wait()
+    mine_theta.wait()
+
+    def forward(side, step, owner):
+        source, target, other = ((REACH, REACH + rows, down), (rows, 0, up))[side]
+        copy = pltpu.make_async_remote_copy(
+            src_ref=wide.at[:, pl.ds(source, REACH), lons(owner), :],
+            dst_ref=wide.at[:, pl.ds(target, REACH), lons(owner), :],
+            send_sem=halo_send.at[side, step], recv_sem=halo_recv.at[side, step],
+            device_id={"lat": other}, device_id_type=MESH)
+        copy.start()
+        return copy
+
+    lower, upper = [forward(0, 0, lon)], [forward(1, 0, lon)]
+
+    def build_row(i, carry):
+        for w in range(WINDOW):
+            for k in range(basis):
+                line = taps[i, pl.ds(w * basis + k, 1), :]
+                turned = pltpu.roll(jnp.broadcast_to(line, (LANES, circle)), 0, 1, stride=1, stride_axis=0)
+                base[i, pl.ds(k * LANES, LANES), pl.ds(w * circle, circle)] = turned.astype(jnp.bfloat16)
+        return carry
+
+    lax.fori_loop(0, rows, build_row, 0)
+
+    owners = [lax.rem(lon + L - step, L) for step in range(L)]
+    for step in range(1, L):
+        sends[0][step - 1].wait_recv()
+        lower.append(forward(0, step, owners[step]))
+    for copy in shared:
+        copy.wait_recv()
+    scale = theta_buf[0]
+    for owner in range(1, L):
+        scale = scale + theta_buf[owner]
+    for step in range(1, L):
+        for row in sends[1:]:
+            row[step - 1].wait_recv()
+        upper.append(forward(1, step, owners[step]))
+    for copy in lower:
+        copy.wait_recv()
+
+    def back(slot, step, e):
+        peer = lax.rem(lon + step, L)
+        return pltpu.make_async_remote_copy(
+            src_ref=staged.at[e, slot, lons(peer), :], dst_ref=got.at[slot, lon * members + e],
+            send_sem=back_send.at[slot, step, e], recv_sem=back_recv.at[slot, step, e],
+            device_id={"lon": peer}, device_id_type=MESH)
+
+    def own(slot, e):
+        return pltpu.make_async_copy(
+            staged.at[e, slot, lons(lon), :], got.at[slot, lon * members + e], own_sem.at[slot, e])
+
+    def send_row(slot):
+        for e in range(members):
+            for step in range(1, L):
+                back(slot, step, e).start()
+            own(slot, e).start()
+
+    def conv_row(slot, carry):
+        i = lax.rem(slot + REACH, rows)
+        for e in range(members):
+            for h in range(circle // LANES):
+                cut = h * LANES
+                pieces = []
+                for w in range(WINDOW):
+                    pieces.append(wide[e, i + w, pl.ds(cut, circle - cut), :])
+                    if cut:
+                        pieces.append(wide[e, i + w, pl.ds(0, cut), :])
+                prod = jnp.dot(base[i], jnp.concatenate(pieces, axis=0), preferred_element_type=jnp.float32)
+                total = prod[:LANES] * scale[0:1, :]
+                for k in range(1, basis):
+                    total = total + prod[k * LANES:(k + 1) * LANES] * scale[k:k + 1, :]
+                staged[e, slot, pl.ds(cut, LANES), :] = total.astype(jnp.bfloat16)
+                if e == 0 and h == 0:
+                    @pl.when(slot > 0)
+                    def _():
+                        send_row(slot - 1)
+        return carry
+
+    first = max(rows - REACH, 0)
+    lax.fori_loop(0, first, conv_row, 0)
+    for copy in upper:
+        copy.wait_recv()
+    lax.fori_loop(first, rows, conv_row, 0)
+    for row in sends:
+        for copy in row:
+            copy.wait_send()
+    for copy in shared + lower + upper:
+        copy.wait_send()
+    bring.wait()
+
+    def mlp_row(slot, carry):
+        i = lax.rem(slot + REACH, rows)
+        for e in range(members):
+            for step in range(1, L):
+                back(slot, step, e).wait_recv()
+            own(slot, e).wait()
+        values = got[slot].reshape(ens * cols, chans).astype(jnp.float32)
+        mean = jnp.mean(values, axis=-1, keepdims=True)
+        diff = values - mean
+        var = jnp.mean(diff * diff, axis=-1, keepdims=True)
+        normed = (diff * lax.rsqrt(var + 1e-05) * gain[...]).astype(jnp.bfloat16)
+        hidden = jnp.dot(normed, w_in[...], preferred_element_type=jnp.float32) + b_in[...]
+        hidden = (0.5 * hidden * (1.0 + lax.erf(hidden * math.sqrt(0.5)))).astype(jnp.bfloat16)
+
+        @pl.when(slot == 0)
+        def _():
+            send_row(rows - 1)
+
+        branch = jnp.dot(hidden, w_out[...], preferred_element_type=jnp.float32)
+        start = held[:, i].reshape(ens * cols, chans).astype(jnp.float32)
+        res[slot] = (start + branch).astype(jnp.bfloat16).reshape(ens, cols, chans)
+
+        @pl.when(slot > 0)
+        def _():
+            before = slot - 1
+            pltpu.make_async_copy(res.at[before], out.at[:, lax.rem(before + REACH, rows)], out_sem.at[before]).start()
+        return carry
+
+    lax.fori_loop(0, rows, mlp_row, 0)
+    pltpu.make_async_copy(res.at[rows - 1], out.at[:, (rows - 1 + REACH) % rows], out_sem.at[rows - 1]).start()
+    for slot in range(rows):
+        for e in range(members):
+            for step in range(1, L):
+                back(slot, step, e).wait_send()
+        pltpu.make_async_copy(res.at[slot], out.at[:, (slot + REACH) % rows], out_sem.at[slot]).wait()
+
+
+def block(fields, theta, taps, gain, w_in, b_in, w_out, L, T):
+    ens, rows, cols, chans = fields.shape
+    members, circle = ens // L, cols * L
+    basis = theta.shape[0]
+    any_space = pl.BlockSpec(memory_space=pl.ANY)
+    vmem = pl.BlockSpec(memory_space=pltpu.VMEM)
+    dma = pltpu.SemaphoreType.DMA
+    bf16 = jnp.bfloat16
+    return pl.pallas_call(
+        functools.partial(block_kernel, L, T, members),
+        out_shape=jax.ShapeDtypeStruct(fields.shape, bf16),
+        in_specs=[any_space] + [vmem] * 6,
+        out_specs=any_space,
+        scratch_shapes=[
+            pltpu.VMEM((members, rows + 2 * REACH, circle, chans), bf16),
+            pltpu.VMEM((rows, basis * LANES, WINDOW * circle), bf16),
+            pltpu.VMEM((L,) + theta.shape, jnp.float32),
+            pltpu.VMEM((members, rows, circle, chans), bf16),
+            pltpu.VMEM((rows, ens, cols, chans), bf16),
+            pltpu.VMEM(fields.shape, bf16),
+            pltpu.VMEM((rows, ens, cols, chans), bf16),
+            dma((2, L)), dma((2, L)), dma((2, L)), dma((2, L)), dma((L,)), dma((L,)), dma((3,)),
+            dma((rows, L, members)), dma((rows, L, members)), dma((rows, members)), dma((rows,)),
+        ],
+        compiler_params=pltpu.CompilerParams(
+            collective_id=0, has_side_effects=True, vmem_limit_bytes=60 * 2**20),
+        name="block",
+    )(fields, theta, taps, gain[None, :], w_in, b_in[None, :], w_out)
 
 
 def with_halo(value, sides, width):
@@ -56,7 +279,7 @@
     return mixed
 
 
-def shards(fields, kernel, theta, row_start, row_count, norm_gain, w_in, b_in, w_out):
+def spectral_shards(fields, kernel, theta, row_start, row_count, norm_gain, w_in, b_in, w_out):
     local = lax.all_to_all(fields, "lon", split_axis=3, concat_axis=2, tiled=True)
     members, band, circle, chans = local.shape
     onward, backward, bins = circle_tables(circle)
@@ -67,7 +290,7 @@
     mixed_im = mix_basis(kern_all[..., bins:], theta)
     first_row = lax.axis_index("lat") * band - REACH
     span_rows = band + 2 * REACH
-    slot_ids = jnp.arange(SLOTS, dtype=jnp.int32)
+    slot_ids = jnp.arange(WINDOW, dtype=jnp.int32)
     offsets = row_start - first_row
     live_slot = slot_ids[None, :] < row_count[:, None]
     total_re = jnp.zeros((members, band, bins, chans), jnp.float32)
@@ -98,6 +321,20 @@
     return (fields.astype(jnp.float32) + branch).astype(jnp.bfloat16)
 
 
+def shards(L, T, fields, kernel, theta, row_start, row_count, norm_gain, w_in, b_in, w_out):
+    if fields.shape[0] % L:
+        return spectral_shards(
+            fields, kernel, theta, row_start, row_count, norm_gain, w_in, b_in, w_out
+        )
+    rows = fields.shape[1]
+    taps = windowed(kernel, row_start, row_count, lax.axis_index("lat") * rows)
+    taps = taps.reshape(rows, -1, taps.shape[-1])
+    chans = theta.shape[1]
+    spread = jnp.zeros((theta.shape[0], chans * L), jnp.float32)
+    spread = lax.dynamic_update_slice(spread, theta, (0, lax.axis_index("lon") * chans))
+    return block(fields, spread, taps, norm_gain, w_in, b_in, w_out, L, T)
+
+
 def solution(mesh):
     placed = (
         P(None, "lat", "lon", None),
@@ -111,5 +348,6 @@
         P(),
     )
     return jax.shard_map(
-        shards, mesh=mesh, in_specs=placed, out_specs=P(None, "lat", "lon", None), check_vma=False
-    )
+        functools.partial(shards, mesh.shape["lon"], mesh.shape["lat"]),
+        mesh=mesh, in_specs=placed, out_specs=P(None, "lat", "lon", None), check_vma=False,
+    )

time: 790 us -> 142 us (0.18); the launches traced: 776 us -> 141 us
  matrix products: 385 us -> 0 us
  local copies, waits for them, and re-layouts: 209 us -> 9.09 us
  Pallas kernels: 0 us -> 130 us
  blocking collectives: 97.3 us -> 0 us
  other arithmetic: 75 us -> 1.68 us
  starting transfers between devices: 8.88 us -> 0 us
    dot_general x38 -> x0, matrix products: 385 us -> none  [the longest x16 159 us: shards(): jnp.einsum('is,isfc->ifc', select, mixed_im, precision=lax.Precision.HIGH...]
    pallas_call x0 -> x1, Pallas kernels: none -> 130 us  [block(): pl.pallas_call(functools.partial(block_kernel, L, T, members), out_shape=...]
    dot_general x32 -> x0, local copies, waits for them, and re-layouts: 119 us -> none  [the longest x16 60 us: shards(): jnp.einsum('is,isfc->ifc', select, mixed_re, precision=lax.Precision.HIGH...]
    all_to_all x1 -> x0, blocking collectives: 97.3 us -> none  [shards(): lax.all_to_all(conv, 'lon', split_axis=2, concat_axis=3, tiled=True)]
    add x2 -> x1, other arithmetic: 36.5 us -> 0.21 us  [windowed(): total + jnp.where(hit[:, :, None, None], kernel[:, slot][:, None], 0.0)]
    convert_element_type x3 -> x0, local copies, waits for them, and re-layouts: 31 us -> none  [the longest x2 23.5 us: shards(): lax.all_to_all(conv, 'lon', split_axis=2, concat_axis=3, tiled=True)]
    sub x2 -> x1, other arithmetic: 28.3 us -> 0.66 us  [windowed(): shift = row_start - (centre - REACH)]
    mul x3 -> x0, local copies, waits for them, and re-layouts: 19.2 us -> none  [the longest x2 19 us: shards(): total_re = total_re + coef_re * row_re - coef_im * row_im]
  transfers between devices with their start and end apart: 3 -> 0, of which waited for: 0 -> 0; matrix products, arithmetic and copies ran while one was open for 57% -> 0% of each run, Pallas kernels for 0% -> 0%
where the time goes in v2:
time: 142 us; the launch traced here: 141 us
  Pallas kernels  130 us (92%)
  local copies, waits for them, and re-layouts  9.09 us (6%)
  other arithmetic  1.68 us (1%)
    pallas_call x1, Pallas kernels, block(): pl.pallas_call(functools.partial(block_kernel, L, T, members), out_shape=...  130 us
    unnamed x5, local copies, waits for them, and re-layouts  3.83 us

profile of v2, /device:TPU:24, one launch (start us, length us, event | category | flops | bytes accessed | tf_op | source)
XLA Modules:
  0.0 140.6 jit_solution(9900881351502634180)
XLA Ops:
  0.0 0.7 add_subtract_fusion
  0.7 1.3 broadcast_in_dim.184.gain
  1.9 0.7 broadcast_compare_fusion.8
  2.6 1.3 broadcast_in_dim.185.b_in
  3.9 0.9 dynamic_update_slice.3.theta
  4.8 0.0 copy-start
  4.8 0.9 slice_bitcast_fusion.8
  5.7 0.2 select_add_fusion
  6.0 0.1 slice.52
  6.1 0.2 reverse.2
  6.3 0.1 slice.62
  6.5 0.1 pad_maximum_fusion
  6.6 0.8 copy.19.taps
  7.4 0.0 copy-done
  7.4 129.7 %block.1 = bf16[4,8,64,640]{3,2,1,0:T(8,128)(2,1)} custom-call(bf16[4,8,64,640]{3,2,1,0:T(8,128)(2,1)} %fields.1, f32[3,640]{1,0:T(4,128)} %copy-done, f32[8,27,256]{2,1,0:T(8,128)} %copy.19.taps, f32[1,640]{1,0:T(1,128)} %broadcast_in_dim.184.gain, bf16[640,1280]{1,0:T(8,128)(2,1)} %w_in.1, f32[1,1280]{1,0:T(1,128)} %broadcast_in_dim.185.b_in, ...), custom_call_target="tpu_custom_call" | custom-call | tf_op jit(solution)/shard_map/block/pallas_call | solution.py:213
  137.1 3.5 %copy.22 = bf16[4,8,64,640]{3,2,1,0:T(8,128)(2,1)} copy(bf16[4,8,64,640]{3,2,1,0:T(8,128)(2,1)} %block.1) | data formatting | bytes 5242880
  (3 shorter events, 0.0 us)
Async XLA Ops:
  4.8 2.6 %copy-start = (f32[3,640]{1,0:T(4,128)}, f32[3,640]{1,0:T(4,128)S(1)}, u32[]{:S(2)}) copy-start(f32[3,640]{1,0:T(4,128)S(1)} %dynamic_update_slice.3.theta) | copy-start | bytes 23044

commit v3 on v2

--- a/solution.py
+++ b/solution.py
@@ -14,31 +14,25 @@
 MESH = pl.DeviceIdType.MESH
 
 
-def windowed(kernel, row_start, row_count, first):
-    rows, slots = kernel.shape[:2]
-    centre = first + jnp.arange(rows, dtype=jnp.int32)
-    shift = row_start - (centre - REACH)
-    place = jnp.arange(WINDOW, dtype=jnp.int32)[None, :] - shift[:, None]
-    total = jnp.zeros((rows, WINDOW) + kernel.shape[2:], jnp.float32)
-    for slot in range(slots):
-        hit = (place == slot) & (slot < row_count[:, None])
-        total = total + jnp.where(hit[:, :, None, None], kernel[:, slot][:, None], 0.0)
-    return jnp.roll(total[..., ::-1], 1, axis=-1)
-
-
 def block_kernel(
-    L, T, members, fields, theta, taps, gain, w_in, b_in, w_out, out,
-    wide, base, theta_buf, staged, got, held, res,
+    L, T, members, fields, theta, kern, starts, counts, gain, w_in_hbm, b_in, w_out_hbm, out,
+    wide, base, taps, w_in, w_out, theta_buf, staged, got, held, res,
     send_sem, recv_sem, halo_send, halo_recv, th_send, th_recv, local_sem, back_send, back_recv, own_sem, out_sem,
 ):
     lat, lon = lax.axis_index("lat"), lax.axis_index("lon")
     up, down = lax.rem(lat + 1, T), lax.rem(lat + T - 1, T)
     ens, rows, cols, chans = held.shape
     circle = wide.shape[2]
-    basis = theta.shape[0]
+    slots, basis = kern.shape[1:3]
 
     bring = pltpu.make_async_copy(fields, held, local_sem.at[2])
     bring.start()
+    weights = [
+        pltpu.make_async_copy(w_in_hbm, w_in, local_sem.at[3]),
+        pltpu.make_async_copy(w_out_hbm, w_out, local_sem.at[4]),
+    ]
+    for copy in weights:
+        copy.start()
     barrier = pltpu.get_barrier_semaphore()
     for step in range(1, L):
         pl.semaphore_signal(barrier, inc=1, device_id={"lon": lax.rem(lon + step, L)}, device_id_type=MESH)
@@ -89,10 +83,22 @@
 
     lower, upper = [forward(0, 0, lon)], [forward(1, 0, lon)]
 
+    place = lax.broadcasted_iota(jnp.int32, (circle, circle), 0) + lax.broadcasted_iota(
+        jnp.int32, (circle, circle), 1)
+    flip = jnp.where((place == 0) | (place == circle), 1.0, 0.0).astype(jnp.bfloat16)
+
     def build_row(i, carry):
+        for s in range(slots):
+            taps[pl.ds(s * basis, basis), :] = kern[i, s]
+        taps[...] = jnp.dot(taps[...].astype(jnp.bfloat16), flip, preferred_element_type=jnp.float32)
+        shift = starts[i] - (lat * rows + i - REACH)
+        count = counts[i]
         for w in range(WINDOW):
+            slot = w - shift
+            live = jnp.where((slot >= 0) & (slot < count), 1.0, 0.0)
+            slot = jnp.clip(slot, 0, slots - 1)
             for k in range(basis):
-                line = taps[i, pl.ds(w * basis + k, 1), :]
+                line = taps[pl.ds(slot * basis + k, 1), :] * live
                 turned = pltpu.roll(jnp.broadcast_to(line, (LANES, circle)), 0, 1, stride=1, stride_axis=0)
                 base[i, pl.ds(k * LANES, LANES), pl.ds(w * circle, circle)] = turned.astype(jnp.bfloat16)
         return carry
@@ -105,9 +111,7 @@
         lower.append(forward(0, step, owners[step]))
     for copy in shared:
         copy.wait_recv()
-    scale = theta_buf[0]
-    for owner in range(1, L):
-        scale = scale + theta_buf[owner]
+    scale = jnp.concatenate([theta_buf[owner] for owner in range(L)], axis=1)
     for step in range(1, L):
         for row in sends[1:]:
             row[step - 1].wait_recv()
@@ -164,6 +168,8 @@
     for copy in shared + lower + upper:
         copy.wait_send()
     bring.wait()
+    for copy in weights:
+        copy.wait()
 
     def mlp_row(slot, carry):
         i = lax.rem(slot + REACH, rows)
@@ -175,8 +181,8 @@
         mean = jnp.mean(values, axis=-1, keepdims=True)
         diff = values - mean
         var = jnp.mean(diff * diff, axis=-1, keepdims=True)
-        normed = (diff * lax.rsqrt(var + 1e-05) * gain[...]).astype(jnp.bfloat16)
-        hidden = jnp.dot(normed, w_in[...], preferred_element_type=jnp.float32) + b_in[...]
+        normed = (diff * lax.rsqrt(var + 1e-05) * gain[...][None, :]).astype(jnp.bfloat16)
+        hidden = jnp.dot(normed, w_in[...], preferred_element_type=jnp.float32) + b_in[...][None, :]
         hidden = (0.5 * hidden * (1.0 + lax.erf(hidden * math.sqrt(0.5)))).astype(jnp.bfloat16)
 
         @pl.when(slot == 0)
@@ -202,34 +208,38 @@
         pltpu.make_async_copy(res.at[slot], out.at[:, (slot + REACH) % rows], out_sem.at[slot]).wait()
 
 
-def block(fields, theta, taps, gain, w_in, b_in, w_out, L, T):
+def block(fields, theta, kern, starts, counts, gain, w_in, b_in, w_out, L, T):
     ens, rows, cols, chans = fields.shape
     members, circle = ens // L, cols * L
     basis = theta.shape[0]
     any_space = pl.BlockSpec(memory_space=pl.ANY)
     vmem = pl.BlockSpec(memory_space=pltpu.VMEM)
+    smem = pl.BlockSpec(memory_space=pltpu.SMEM)
     dma = pltpu.SemaphoreType.DMA
     bf16 = jnp.bfloat16
     return pl.pallas_call(
         functools.partial(block_kernel, L, T, members),
         out_shape=jax.ShapeDtypeStruct(fields.shape, bf16),
-        in_specs=[any_space] + [vmem] * 6,
+        in_specs=[any_space, vmem, vmem, smem, smem, vmem, any_space, vmem, any_space],
         out_specs=any_space,
         scratch_shapes=[
             pltpu.VMEM((members, rows + 2 * REACH, circle, chans), bf16),
             pltpu.VMEM((rows, basis * LANES, WINDOW * circle), bf16),
+            pltpu.VMEM((kern.shape[1] * basis, circle), jnp.float32),
+            pltpu.VMEM(w_in.shape, bf16),
+            pltpu.VMEM(w_out.shape, bf16),
             pltpu.VMEM((L,) + theta.shape, jnp.float32),
             pltpu.VMEM((members, rows, circle, chans), bf16),
             pltpu.VMEM((rows, ens, cols, chans), bf16),
             pltpu.VMEM(fields.shape, bf16),
             pltpu.VMEM((rows, ens, cols, chans), bf16),
-            dma((2, L)), dma((2, L)), dma((2, L)), dma((2, L)), dma((L,)), dma((L,)), dma((3,)),
+            dma((2, L)), dma((2, L)), dma((2, L)), dma((2, L)), dma((L,)), dma((L,)), dma((5,)),
             dma((rows, L, members)), dma((rows, L, members)), dma((rows, members)), dma((rows,)),
         ],
         compiler_params=pltpu.CompilerParams(
-            collective_id=0, has_side_effects=True, vmem_limit_bytes=60 * 2**20),
+            collective_id=0, has_side_effects=True, vmem_limit_bytes=46 * 2**20),
         name="block",
-    )(fields, theta, taps, gain[None, :], w_in, b_in[None, :], w_out)
+    )(fields, theta, kern, starts, counts, gain, w_in, b_in, w_out)
 
 
 def with_halo(value, sides, width):
@@ -326,13 +336,7 @@
         return spectral_shards(
             fields, kernel, theta, row_start, row_count, norm_gain, w_in, b_in, w_out
         )
-    rows = fields.shape[1]
-    taps = windowed(kernel, row_start, row_count, lax.axis_index("lat") * rows)
-    taps = taps.reshape(rows, -1, taps.shape[-1])
-    chans = theta.shape[1]
-    spread = jnp.zeros((theta.shape[0], chans * L), jnp.float32)
-    spread = lax.dynamic_update_slice(spread, theta, (0, lax.axis_index("lon") * chans))
-    return block(fields, spread, taps, norm_gain, w_in, b_in, w_out, L, T)
+    return block(fields, theta, kernel, row_start, row_count, norm_gain, w_in, b_in, w_out, L, T)
 
 
 def solution(mesh):

time: 142 us -> 138 us (0.972)
  Pallas kernels: 130 us -> 127 us
  other arithmetic: 1.68 us -> 0 us
    unnamed x5 -> x16, local copies, waits for them, and re-layouts: 3.83 us -> 8.78 us
    broadcast_in_dim x4 -> x0, local copies, waits for them, and re-layouts: 3.48 us -> none  [the longest x1 1.29 us: block(): b_in[None, :]]
    pallas_call x1, Pallas kernels: 130 us -> 127 us  [block(): pl.pallas_call(functools.partial(block_kernel, L, T, members), out_shape=...]
where the time goes in v3:
time: 138 us; the launch traced here: 136 us
  Pallas kernels  127 us (92%)
  local copies, waits for them, and re-layouts  8.78 us (6%)
    pallas_call x1, Pallas kernels, block(): pl.pallas_call(functools.partial(block_kernel, L, T, members), out_shape=...  127 us
    unnamed x16, local copies, waits for them, and re-layouts  8.78 us

profile of v3, /device:TPU:24, one launch (start us, length us, event | category | flops | bytes accessed | tf_op | source)
XLA Modules:
  0.0 136.2 jit_solution(12414430303495664671)
XLA Ops:
  0.0 1.1 copy.10.kern
  1.1 0.0 copy-start
  1.1 1.4 %copy-done = bf16[640,1280]{1,0:T(8,128)(2,1)S(1)} copy-done((bf16[640,1280]{1,0:T(8,128)(2,1)S(1)}, bf16[640,1280]{1,0:T(8,128)(2,1)}, u32[]{:S(2)}) %copy-start) | copy-done | bytes 1638424
  2.5 0.0 copy-start.1
  2.5 1.4 %copy-done.1 = bf16[1280,640]{1,0:T(8,128)(2,1)S(1)} copy-done((bf16[1280,640]{1,0:T(8,128)(2,1)S(1)}, bf16[1280,640]{1,0:T(8,128)(2,1)}, u32[]{:S(2)}) %copy-start.1) | copy-done | bytes 1638424
  3.9 0.0 copy-start.2
  3.9 0.7 copy-done.2
  4.6 0.0 copy-start.3
  4.6 0.7 copy-done.3
  5.3 0.0 copy-start.4
  5.3 0.7 copy-done.4
  6.0 0.0 copy-start.5
  6.0 0.7 copy-done.5
  6.6 0.0 copy-start.6
  6.6 0.7 copy-done.6
  7.3 127.4 %block.1 = bf16[4,8,64,640]{3,2,1,0:T(8,128)(2,1)S(1)} custom-call(bf16[4,8,64,640]{3,2,1,0:T(8,128)(2,1)} %fields.1, f32[3,160]{1,0:T(4,128)S(1)} %copy-done.3, f32[8,9,3,256]{3,2,1,0:T(4,128)S(1)} %copy.10.kern, s32[8]{0:T(128)S(1)} %copy-done.5, s32[8]{0:T(128)S(1)} %copy-done.6, f32[640]{0:T(1024)S(1)} %copy-done.4, bf16[640,1280]{1,0:T(8,128)(2,1)S(1)} %copy-done, ...), custom_call_target="tpu_custom_call" | custom-call | tf_op jit(solution)/shard_map/block/pallas_call | solution.py:220
  134.8 1.5 %copy.12 = bf16[4,8,64,640]{3,2,1,0:T(8,128)(2,1)} copy(bf16[4,8,64,640]{3,2,1,0:T(8,128)(2,1)S(1)} %block.1) | data formatting | bytes 5242880
Async XLA Ops:
  1.1 1.4 %copy-start = (bf16[640,1280]{1,0:T(8,128)(2,1)S(1)}, bf16[640,1280]{1,0:T(8,128)(2,1)}, u32[]{:S(2)}) copy-start(bf16[640,1280]{1,0:T(8,128)(2,1)} %w_in_hbm.1) | copy-start | bytes 4915204
  2.5 1.4 %copy-start.1 = (bf16[1280,640]{1,0:T(8,128)(2,1)S(1)}, bf16[1280,640]{1,0:T(8,128)(2,1)}, u32[]{:S(2)}) copy-start(bf16[1280,640]{1,0:T(8,128)(2,1)} %w_out_hbm.1) | copy-start | bytes 4915204
  3.9 0.7 copy-start.2
  4.6 0.7 copy-start.3
  5.3 0.7 copy-start.4
  6.0 0.7 copy-start.5
  6.6 0.7 copy-start.6

commit v4 on v3

--- a/solution.py
+++ b/solution.py
@@ -15,23 +15,22 @@
 
 
 def block_kernel(
-    L, T, members, fields, theta, kern, starts, counts, gain, w_in_hbm, b_in, w_out_hbm, out,
-    wide, base, taps, w_in, w_out, theta_buf, staged, got, held, res,
+    L, T, members, fields, theta, kern_hbm, starts_hbm, counts_hbm, gain_hbm, w_in_hbm, b_in_hbm, w_out_hbm, out,
+    wide, base, taps, kern, starts, counts, gain, w_in, b_in, w_out, theta_buf, staged, got, held, res,
     send_sem, recv_sem, halo_send, halo_recv, th_send, th_recv, local_sem, back_send, back_recv, own_sem, out_sem,
 ):
     lat, lon = lax.axis_index("lat"), lax.axis_index("lon")
     up, down = lax.rem(lat + 1, T), lax.rem(lat + T - 1, T)
     ens, rows, cols, chans = held.shape
     circle = wide.shape[2]
-    slots, basis = kern.shape[1:3]
+    slots, basis = kern.shape[:2]
 
     bring = pltpu.make_async_copy(fields, held, local_sem.at[2])
     bring.start()
-    weights = [
-        pltpu.make_async_copy(w_in_hbm, w_in, local_sem.at[3]),
-        pltpu.make_async_copy(w_out_hbm, w_out, local_sem.at[4]),
-    ]
-    for copy in weights:
+    pairs = ((kern_hbm, kern), (starts_hbm, starts), (counts_hbm, counts), (gain_hbm, gain),
+             (w_in_hbm, w_in), (b_in_hbm, b_in), (w_out_hbm, w_out))
+    loads = [pltpu.make_async_copy(a, b, local_sem.at[3 + n]) for n, (a, b) in enumerate(pairs)]
+    for copy in loads:
         copy.start()
     barrier = pltpu.get_barrier_semaphore()
     for step in range(1, L):
@@ -87,10 +86,12 @@
         jnp.int32, (circle, circle), 1)
     flip = jnp.where((place == 0) | (place == circle), 1.0, 0.0).astype(jnp.bfloat16)
 
+    for copy in loads[:3]:
+        copy.wait()
+    profiles = kern[...].reshape(slots * basis * rows, circle).astype(jnp.bfloat16)
+    taps[...] = jnp.dot(profiles, flip, preferred_element_type=jnp.float32)
+
     def build_row(i, carry):
-        for s in range(slots):
-            taps[pl.ds(s * basis, basis), :] = kern[i, s]
-        taps[...] = jnp.dot(taps[...].astype(jnp.bfloat16), flip, preferred_element_type=jnp.float32)
         shift = starts[i] - (lat * rows + i - REACH)
         count = counts[i]
         for w in range(WINDOW):
@@ -98,7 +99,7 @@
             live = jnp.where((slot >= 0) & (slot < count), 1.0, 0.0)
             slot = jnp.clip(slot, 0, slots - 1)
             for k in range(basis):
-                line = taps[pl.ds(slot * basis + k, 1), :] * live
+                line = taps[pl.ds((slot * basis + k) * rows + i, 1), :] * live
                 turned = pltpu.roll(jnp.broadcast_to(line, (LANES, circle)), 0, 1, stride=1, stride_axis=0)
                 base[i, pl.ds(k * LANES, LANES), pl.ds(w * circle, circle)] = turned.astype(jnp.bfloat16)
         return carry
@@ -168,7 +169,7 @@
     for copy in shared + lower + upper:
         copy.wait_send()
     bring.wait()
-    for copy in weights:
+    for copy in loads[3:]:
         copy.wait()
 
     def mlp_row(slot, carry):
@@ -213,31 +214,34 @@
     members, circle = ens // L, cols * L
     basis = theta.shape[0]
     any_space = pl.BlockSpec(memory_space=pl.ANY)
-    vmem = pl.BlockSpec(memory_space=pltpu.VMEM)
-    smem = pl.BlockSpec(memory_space=pltpu.SMEM)
     dma = pltpu.SemaphoreType.DMA
     bf16 = jnp.bfloat16
     return pl.pallas_call(
         functools.partial(block_kernel, L, T, members),
         out_shape=jax.ShapeDtypeStruct(fields.shape, bf16),
-        in_specs=[any_space, vmem, vmem, smem, smem, vmem, any_space, vmem, any_space],
+        in_specs=[pl.BlockSpec(memory_space=pltpu.HBM)] * 9,
         out_specs=any_space,
         scratch_shapes=[
             pltpu.VMEM((members, rows + 2 * REACH, circle, chans), bf16),
             pltpu.VMEM((rows, basis * LANES, WINDOW * circle), bf16),
-            pltpu.VMEM((kern.shape[1] * basis, circle), jnp.float32),
+            pltpu.VMEM((kern.shape[0] * basis * rows, circle), jnp.float32),
+            pltpu.VMEM(kern.shape, jnp.float32),
+            pltpu.SMEM(starts.shape, jnp.int32),
+            pltpu.SMEM(counts.shape, jnp.int32),
+            pltpu.VMEM(gain.shape, jnp.float32),
             pltpu.VMEM(w_in.shape, bf16),
+            pltpu.VMEM(b_in.shape, jnp.float32),
             pltpu.VMEM(w_out.shape, bf16),
             pltpu.VMEM((L,) + theta.shape, jnp.float32),
             pltpu.VMEM((members, rows, circle, chans), bf16),
             pltpu.VMEM((rows, ens, cols, chans), bf16),
             pltpu.VMEM(fields.shape, bf16),
             pltpu.VMEM((rows, ens, cols, chans), bf16),
-            dma((2, L)), dma((2, L)), dma((2, L)), dma((2, L)), dma((L,)), dma((L,)), dma((5,)),
+            dma((2, L)), dma((2, L)), dma((2, L)), dma((2, L)), dma((L,)), dma((L,)), dma((10,)),
             dma((rows, L, members)), dma((rows, L, members)), dma((rows, members)), dma((rows,)),
         ],
         compiler_params=pltpu.CompilerParams(
-            collective_id=0, has_side_effects=True, vmem_limit_bytes=46 * 2**20),
+            collective_id=0, has_side_effects=True, vmem_limit_bytes=58 * 2**20),
         name="block",
     )(fields, theta, kern, starts, counts, gain, w_in, b_in, w_out)
 
@@ -336,7 +340,8 @@
         return spectral_shards(
             fields, kernel, theta, row_start, row_count, norm_gain, w_in, b_in, w_out
         )
-    return block(fields, theta, kernel, row_start, row_count, norm_gain, w_in, b_in, w_out, L, T)
+    kern = jnp.transpose(kernel, (1, 2, 0, 3))
+    return block(fields, theta, kern, row_start, row_count, norm_gain, w_in, b_in, w_out, L, T)
 
 
 def solution(mesh):

time: 138 us -> 133 us (0.964)
  local copies, waits for them, and re-layouts: 8.78 us -> 3.47 us
    unnamed x16 -> x1, local copies, waits for them, and re-layouts: 8.78 us -> 3.47 us
where the time goes in v4:
time: 133 us; the launch traced here: 131 us
  Pallas kernels  127 us (95%)
  local copies, waits for them, and re-layouts  3.47 us (3%)
    pallas_call x1, Pallas kernels, block(): pl.pallas_call(functools.partial(block_kernel, L, T, members), out_shape=...  127 us
    unnamed x1, local copies, waits for them, and re-layouts  3.47 us

profile of v4, /device:TPU:24, one launch (start us, length us, event | category | flops | bytes accessed | tf_op | source)
XLA Modules:
  0.0 130.7 jit_solution(611442750663864745)
XLA Ops:
  0.0 127.3 %block.1 = bf16[4,8,64,640]{3,2,1,0:T(8,128)(2,1)} custom-call(bf16[4,8,64,640]{3,2,1,0:T(8,128)(2,1)} %fields.1, f32[3,160]{1,0:T(4,128)} %theta.1, f32[9,3,8,256]{3,2,1,0:T(8,128)} %bitcast.1, s32[8]{0:T(128)} %starts_hbm.1, s32[8]{0:T(128)} %counts_hbm.1, f32[640]{0:T(1024)} %gain_hbm.1, bf16[640,1280]{1,0:T(8,128)(2,1)} %w_in_hbm.1, f32[1280]{0:T(1024)} %b_in_hbm.1, ...), custom_call_target="tpu_custom_call" | custom-call | tf_op jit(solution)/shard_map/block/pallas_call | solution.py:219
  127.3 3.5 %copy.11 = bf16[4,8,64,640]{3,2,1,0:T(8,128)(2,1)} copy(bf16[4,8,64,640]{3,2,1,0:T(8,128)(2,1)} %block.1) | data formatting | bytes 5242880

commit v5 on v4

--- a/solution.py
+++ b/solution.py
@@ -43,18 +43,23 @@
         return pl.ds(pl.multiple_of(owner * cols, cols), cols)
 
     chunks = [(0, REACH)] + ([(REACH, rows - REACH)] if rows > REACH else [])
+    split = (chans - 1) // LANES * LANES
+    parts = [(0, split), (split, chans - split)] if split else [(0, chans)]
     sends = []
-    for c, (low, size) in enumerate(chunks):
-        row = []
-        for step in range(1, L):
-            peer = lax.rem(lon + step, L)
-            row.append(pltpu.make_async_remote_copy(
-                src_ref=fields.at[pl.ds(peer * members, members), pl.ds(low, size)],
-                dst_ref=wide.at[:, pl.ds(REACH + low, size), lons(lon), :],
-                send_sem=send_sem.at[c, step], recv_sem=recv_sem.at[c, step],
-                device_id={"lon": peer}, device_id_type=MESH))
-            row[-1].start()
-        sends.append(row)
+    for g, (first_chan, width) in enumerate(parts):
+        sends.append([])
+        for c, (low, size) in enumerate(chunks):
+            row = []
+            for step in range(1, L):
+                peer = lax.rem(lon + step, L)
+                row.append(pltpu.make_async_remote_copy(
+                    src_ref=fields.at[
+                        pl.ds(peer * members, members), pl.ds(low, size), :, pl.ds(first_chan, width)],
+                    dst_ref=wide.at[:, pl.ds(REACH + low, size), lons(lon), pl.ds(first_chan, width)],
+                    send_sem=send_sem.at[2 * g + c, step], recv_sem=recv_sem.at[2 * g + c, step],
+                    device_id={"lon": peer}, device_id_type=MESH))
+                row[-1].start()
+            sends[-1].append(row)
     shared = []
     for step in range(1, L):
         shared.append(pltpu.make_async_remote_copy(
@@ -70,17 +75,19 @@
     mine.wait()
     mine_theta.wait()
 
-    def forward(side, step, owner):
+    def forward(side, g, step, owner):
         source, target, other = ((REACH, REACH + rows, down), (rows, 0, up))[side]
+        chan = pl.ds(*parts[g])
         copy = pltpu.make_async_remote_copy(
-            src_ref=wide.at[:, pl.ds(source, REACH), lons(owner), :],
-            dst_ref=wide.at[:, pl.ds(target, REACH), lons(owner), :],
-            send_sem=halo_send.at[side, step], recv_sem=halo_recv.at[side, step],
+            src_ref=wide.at[:, pl.ds(source, REACH), lons(owner), chan],
+            dst_ref=wide.at[:, pl.ds(target, REACH), lons(owner), chan],
+            send_sem=halo_send.at[2 * g + side, step], recv_sem=halo_recv.at[2 * g + side, step],
             device_id={"lat": other}, device_id_type=MESH)
         copy.start()
         return copy
 
-    lower, upper = [forward(0, 0, lon)], [forward(1, 0, lon)]
+    lower = [[forward(0, g, 0, lon)] for g in range(len(parts))]
+    upper = [[forward(1, g, 0, lon)] for g in range(len(parts))]
 
     place = lax.broadcasted_iota(jnp.int32, (circle, circle), 0) + lax.broadcasted_iota(
         jnp.int32, (circle, circle), 1)
@@ -107,18 +114,21 @@
     lax.fori_loop(0, rows, build_row, 0)
 
     owners = [lax.rem(lon + L - step, L) for step in range(L)]
-    for step in range(1, L):
-        sends[0][step - 1].wait_recv()
-        lower.append(forward(0, step, owners[step]))
+
+    def arrive(g):
+        for step in range(1, L):
+            sends[g][0][step - 1].wait_recv()
+            lower[g].append(forward(0, g, step, owners[step]))
+        for step in range(1, L):
+            for row in sends[g][1:]:
+                row[step - 1].wait_recv()
+            upper[g].append(forward(1, g, step, owners[step]))
+        for copy in lower[g]:
+            copy.wait_recv()
+
     for copy in shared:
         copy.wait_recv()
     scale = jnp.concatenate([theta_buf[owner] for owner in range(L)], axis=1)
-    for step in range(1, L):
-        for row in sends[1:]:
-            row[step - 1].wait_recv()
-        upper.append(forward(1, step, owners[step]))
-    for copy in lower:
-        copy.wait_recv()
 
     def back(slot, step, e):
         peer = lax.rem(lon + step, L)
@@ -137,36 +147,39 @@
                 back(slot, step, e).start()
             own(slot, e).start()
 
-    def conv_row(slot, carry):
+    def conv_row(first_chan, width, sending, slot, carry):
+        chan = pl.ds(first_chan, width)
         i = lax.rem(slot + REACH, rows)
         for e in range(members):
             for h in range(circle // LANES):
                 cut = h * LANES
                 pieces = []
                 for w in range(WINDOW):
-                    pieces.append(wide[e, i + w, pl.ds(cut, circle - cut), :])
+                    pieces.append(wide[e, i + w, pl.ds(cut, circle - cut), chan])
                     if cut:
-                        pieces.append(wide[e, i + w, pl.ds(0, cut), :])
+                        pieces.append(wide[e, i + w, pl.ds(0, cut), chan])
                 prod = jnp.dot(base[i], jnp.concatenate(pieces, axis=0), preferred_element_type=jnp.float32)
-                total = prod[:LANES] * scale[0:1, :]
+                total = prod[:LANES] * scale[0:1, first_chan:first_chan + width]
                 for k in range(1, basis):
-                    total = total + prod[k * LANES:(k + 1) * LANES] * scale[k:k + 1, :]
-                staged[e, slot, pl.ds(cut, LANES), :] = total.astype(jnp.bfloat16)
-                if e == 0 and h == 0:
+                    total = total + prod[k * LANES:(k + 1) * LANES] * scale[k:k + 1, first_chan:first_chan + width]
+                staged[e, slot, pl.ds(cut, LANES), chan] = total.astype(jnp.bfloat16)
+                if sending and e == 0 and h == 0:
                     @pl.when(slot > 0)
                     def _():
                         send_row(slot - 1)
         return carry
 
     first = max(rows - REACH, 0)
-    lax.fori_loop(0, first, conv_row, 0)
-    for copy in upper:
+    for g, part in enumerate(parts):
+        arrive(g)
+        lax.fori_loop(0, first, functools.partial(conv_row, *part, g == len(parts) - 1), 0)
+    for copy in sum(upper, []):
         copy.wait_recv()
-    lax.fori_loop(first, rows, conv_row, 0)
-    for row in sends:
+    lax.fori_loop(first, rows, functools.partial(conv_row, 0, chans, True), 0)
+    for row in sum(sends, []):
         for copy in row:
             copy.wait_send()
-    for copy in shared + lower + upper:
+    for copy in shared + sum(lower + upper, []):
         copy.wait_send()
     bring.wait()
     for copy in loads[3:]:
@@ -237,7 +250,7 @@
             pltpu.VMEM((rows, ens, cols, chans), bf16),
             pltpu.VMEM(fields.shape, bf16),
             pltpu.VMEM((rows, ens, cols, chans), bf16),
-            dma((2, L)), dma((2, L)), dma((2, L)), dma((2, L)), dma((L,)), dma((L,)), dma((10,)),
+            dma((4, L)), dma((4, L)), dma((4, L)), dma((4, L)), dma((L,)), dma((L,)), dma((10,)),
             dma((rows, L, members)), dma((rows, L, members)), dma((rows, members)), dma((rows,)),
         ],
         compiler_params=pltpu.CompilerParams(

time: 133 us -> 157 us (1.18)
  Pallas kernels: 127 us -> 152 us
    pallas_call x1, Pallas kernels: 127 us -> 152 us  [block(): pl.pallas_call(functools.partial(block_kernel, L, T, members), out_shape=...]
where the time goes in v5:
time: 157 us; the launch traced here: 156 us
  Pallas kernels  152 us (97%)
  local copies, waits for them, and re-layouts  3.47 us (2%)
    pallas_call x1, Pallas kernels, block(): pl.pallas_call(functools.partial(block_kernel, L, T, members), out_shape=...  152 us
    unnamed x1, local copies, waits for them, and re-layouts  3.47 us

profile of v5, /device:TPU:24, one launch (start us, length us, event | category | flops | bytes accessed | tf_op | source)
XLA Modules:
  0.0 155.6 jit_solution(5781938695422612844)
XLA Ops:
  0.0 152.1 %block.1 = bf16[4,8,64,640]{3,2,1,0:T(8,128)(2,1)} custom-call(bf16[4,8,64,640]{3,2,1,0:T(8,128)(2,1)} %fields.1, f32[3,160]{1,0:T(4,128)} %theta.1, f32[9,3,8,256]{3,2,1,0:T(8,128)} %bitcast.1, s32[8]{0:T(128)} %starts_hbm.1, s32[8]{0:T(128)} %counts_hbm.1, f32[640]{0:T(1024)} %gain_hbm.1, bf16[640,1280]{1,0:T(8,128)(2,1)} %w_in_hbm.1, f32[1280]{0:T(1024)} %b_in_hbm.1, ...), custom_call_target="tpu_custom_call" | custom-call | tf_op jit(solution)/shard_map/block/pallas_call | solution.py:232
  152.1 3.5 %copy.11 = bf16[4,8,64,640]{3,2,1,0:T(8,128)(2,1)} copy(bf16[4,8,64,640]{3,2,1,0:T(8,128)(2,1)} %block.1) | data formatting | bytes 5242880

commit v6 on v4

--- a/solution.py
+++ b/solution.py
@@ -131,11 +131,20 @@
         return pltpu.make_async_copy(
             staged.at[e, slot, lons(lon), :], got.at[slot, lon * members + e], own_sem.at[slot, e])
 
-    def send_row(slot):
-        for e in range(members):
-            for step in range(1, L):
-                back(slot, step, e).start()
-            own(slot, e).start()
+    blocks = circle // LANES
+
+    def send_part(slot, h):
+        for step in range(1, L):
+            peer = lax.rem(lon + step, L)
+
+            @pl.when((peer * cols + cols - 1) // LANES == h)
+            def _():
+                for e in range(members):
+                    back(slot, step, e).start()
+
+        if h == blocks - 1:
+            for e in range(members):
+                own(slot, e).start()
 
     def conv_row(slot, carry):
         i = lax.rem(slot + REACH, rows)
@@ -152,10 +161,12 @@
                 for k in range(1, basis):
                     total = total + prod[k * LANES:(k + 1) * LANES] * scale[k:k + 1, :]
                 staged[e, slot, pl.ds(cut, LANES), :] = total.astype(jnp.bfloat16)
+                if e == members - 1 and h > 0:
+                    send_part(slot, h - 1)
                 if e == 0 and h == 0:
                     @pl.when(slot > 0)
                     def _():
-                        send_row(slot - 1)
+                        send_part(slot - 1, blocks - 1)
         return carry
 
     first = max(rows - REACH, 0)
@@ -188,7 +199,7 @@
 
         @pl.when(slot == 0)
         def _():
-            send_row(rows - 1)
+            send_part(rows - 1, blocks - 1)
 
         branch = jnp.dot(hidden, w_out[...], preferred_element_type=jnp.float32)
         start = held[:, i].reshape(ens * cols, chans).astype(jnp.float32)

time: 133 us -> 131 us (0.985); the launches traced: 131 us -> 131 us
  no operation moved by 1% of the time
where the time goes in v6:
time: 131 us
  Pallas kernels  127 us (97%)
  local copies, waits for them, and re-layouts  3.47 us (3%)
    pallas_call x1, Pallas kernels, block(): pl.pallas_call(functools.partial(block_kernel, L, T, members), out_shape=...  127 us
    unnamed x1, local copies, waits for them, and re-layouts  3.47 us

profile of v6, /device:TPU:24, one launch (start us, length us, event | category | flops | bytes accessed | tf_op | source)
XLA Modules:
  0.0 130.7 jit_solution(1945967176947402506)
XLA Ops:
  0.0 127.3 %block.1 = bf16[4,8,64,640]{3,2,1,0:T(8,128)(2,1)} custom-call(bf16[4,8,64,640]{3,2,1,0:T(8,128)(2,1)} %fields.1, f32[3,160]{1,0:T(4,128)} %theta.1, f32[9,3,8,256]{3,2,1,0:T(8,128)} %bitcast.1, s32[8]{0:T(128)} %starts_hbm.1, s32[8]{0:T(128)} %counts_hbm.1, f32[640]{0:T(1024)} %gain_hbm.1, bf16[640,1280]{1,0:T(8,128)(2,1)} %w_in_hbm.1, f32[1280]{0:T(1024)} %b_in_hbm.1, ...), custom_call_target="tpu_custom_call" | custom-call | tf_op jit(solution)/shard_map/block/pallas_call | solution.py:230
  127.3 3.5 %copy.11 = bf16[4,8,64,640]{3,2,1,0:T(8,128)(2,1)} copy(bf16[4,8,64,640]{3,2,1,0:T(8,128)(2,1)} %block.1) | data formatting | bytes 5242880
